TPU v7x, 512 devices: a whole 4x4x16 slice. The times are simulated.
512 devices in a mesh: dp: 64 (over x, y, z_hi, core), shard: 8 (over z_lo).
Axes of the slice: x: 4, y: 4, z: 16 (z_hi: 2, z_lo: 8; z = z_hi * 8 + z_lo), core: 2. Of those that a mesh axis runs over, the one named last changes fastest.
Arguments:
- group_grads: bfloat16 [64, 1024, 1024], P('dp', 'shard'), may hold values from -2 to 2
- moment: float32 [1024, 1024], P('shard'), may hold values from -6 to 6
- second: float32 [1024, 1024], P(None, 'shard'), may hold values from 0.5 to 4
- stat_left: float32 [1024, 1024], P('shard'), may hold values from -200 to 2000, as said below
- stat_right: float32 [1024, 1024], P('shard'), may hold values from -200 to 2000, as said below
- basis_left: float32 [1024, 1024], P('shard'), as said below
- basis_right: float32 [1024, 1024], P('shard'), as said below
Outputs:
- update: bfloat16 [1024, 1024], P('shard')
- second_new: float32 [1024, 1024], P(None, 'shard')
- left_new: float32 [1024, 1024], P('shard')
- right_new: float32 [1024, 1024], P('shard')
Inputs may be any that keep to these rules, and one draw needn't show every extreme that they name: `stat_left`: each statistic is symmetric. `stat_right`: each statistic is symmetric. `basis_left`: diagonal entries near 0.9 sqrt(1024), off-diagonal entries of order one. `basis_right`: diagonal entries near 0.9 sqrt(1024), off-diagonal entries of order one.
All inputs are finite; a program needn't handle non-finite values.
Results may differ from a plain program's by a relative error of at most 0.0049.
The roundings to bfloat16 on the way count: a program that leaves them out, or rounds other values in their place, can miss the bound.
Values may be sent and summed in bfloat16 or wider, within the bound.
A program may use at most 128 MiB of HBM per device.

v0:
```python
import jax
import jax.numpy as jnp
from jax import lax
from jax.sharding import PartitionSpec as P

NS_ITERS = 2


BETA_ONE = 0.9
BETA_TWO = 0.9
BETA_STAT = 0.95
EPSILON = 1e-08
NORM_EPS = 1e-06


def contract_rows(left_mat, right_mat):
    return lax.dot_general(
        left_mat, right_mat, (((0,), (0,)), ((), ())), preferred_element_type=jnp.float32
    )


def contract_cols(left_mat, right_mat):
    return lax.dot_general(
        left_mat, right_mat, (((1,), (1,)), ((), ())), preferred_element_type=jnp.float32
    )


def body(group_grads, moment, second, stat_left, stat_right, basis_left, basis_right):
    position = lax.axis_index("shard")
    row_count = moment.shape[0]
    block_width = moment.shape[1]
    local_sum = group_grads[0].astype(jnp.float32)
    summed = lax.psum(local_sum, "dp")
    grad_rows = summed.astype(jnp.bfloat16)
    gradient = lax.all_gather(grad_rows, "shard", axis=0, tiled=True)
    moment_half = (BETA_ONE * moment + (1.0 - BETA_ONE) * grad_rows.astype(jnp.float32)).astype(
        jnp.bfloat16
    )
    left_stat = BETA_STAT * stat_left + (1.0 - BETA_STAT) * contract_cols(grad_rows, gradient)
    grad_cols = lax.dynamic_slice_in_dim(gradient, position * row_count, row_count, 1)
    right_stat = BETA_STAT * stat_right + (1.0 - BETA_STAT) * contract_rows(grad_cols, gradient)
    left_rot, right_rot = (
        lax.all_gather(basis_left.astype(jnp.bfloat16), "shard", axis=0, tiled=True),
        lax.all_gather(basis_right.astype(jnp.bfloat16), "shard", axis=0, tiled=True),
    )
    grad_turned = jnp.dot(grad_rows, right_rot, preferred_element_type=jnp.float32).astype(
        jnp.bfloat16
    )
    moment_turned = jnp.dot(moment_half, right_rot, preferred_element_type=jnp.float32).astype(
        jnp.bfloat16
    )
    grad_block, moment_block = (
        lax.all_to_all(grad_turned, "shard", split_axis=1, concat_axis=0, tiled=True),
        lax.all_to_all(moment_turned, "shard", split_axis=1, concat_axis=0, tiled=True),
    )
    grad_rot = contract_rows(left_rot, grad_block) / block_width
    moment_rot = contract_rows(left_rot, moment_block) / block_width
    second_new = BETA_TWO * second + (1.0 - BETA_TWO) * grad_rot * grad_rot
    scaled = (moment_rot / (jnp.sqrt(second_new) + EPSILON)).astype(jnp.bfloat16)
    turned_back = jnp.dot(left_rot, scaled, preferred_element_type=jnp.float32).astype(jnp.bfloat16)
    back_rows = lax.all_to_all(turned_back, "shard", split_axis=0, concat_axis=1, tiled=True)
    update = (contract_cols(back_rows, right_rot) / block_width).astype(jnp.bfloat16)
    left_product = jnp.dot(
        left_stat.astype(jnp.bfloat16), left_rot, preferred_element_type=jnp.float32
    )
    right_product = jnp.dot(
        right_stat.astype(jnp.bfloat16), right_rot, preferred_element_type=jnp.float32
    )
    left_sq, right_sq = lax.psum(
        (
            jnp.sum(left_product * left_product, axis=0),
            jnp.sum(right_product * right_product, axis=0),
        ),
        "shard",
    )
    left_start = left_product / jnp.sqrt(left_sq / block_width + NORM_EPS)
    right_start = right_product / jnp.sqrt(right_sq / block_width + NORM_EPS)
    left_current = left_start.astype(jnp.bfloat16)
    right_current = right_start.astype(jnp.bfloat16)
    left_result = left_start
    right_result = right_start
    for iteration in range(NS_ITERS):
        left_full, right_full = (
            lax.all_gather(left_current, "shard", axis=0, tiled=True),
            lax.all_gather(right_current, "shard", axis=0, tiled=True),
        )
        left_gram = (contract_cols(left_current, left_full) / block_width).astype(jnp.bfloat16)
        right_gram = (contract_cols(right_current, right_full) / block_width).astype(jnp.bfloat16)
        left_result = 1.5 * left_current.astype(jnp.float32) - 0.5 * jnp.dot(
            left_gram, left_full, preferred_element_type=jnp.float32
        )
        right_result = 1.5 * right_current.astype(jnp.float32) - 0.5 * jnp.dot(
            right_gram, right_full, preferred_element_type=jnp.float32
        )
        if iteration + 1 < NS_ITERS:
            left_current = left_result.astype(jnp.bfloat16)
            right_current = right_result.astype(jnp.bfloat16)
    return (update, second_new, left_result, right_result)


def solution(mesh):
    return jax.shard_map(
        body,
        mesh=mesh,
        in_specs=(
            P("dp", "shard", None),
            P("shard", None),
            P(None, "shard"),
            P("shard", None),
            P("shard", None),
            P("shard", None),
            P("shard", None),
        ),
        out_specs=(P("shard", None), P(None, "shard"), P("shard", None), P("shard", None)),
        check_vma=False,
    )
```

profile of v0, /device:TPU:1, one launch (start us, length us, event | category | flops | bytes accessed | tf_op | source)
XLA Modules:
  0.0 1039.4 jit_solution(8911821349268861389)
XLA Ops:
  7.2 1.9 convert_element_type.88
  9.2 1.0 bitcast_convert_fusion
  10.2 561.8 %all-reduce.2 = bf16[128,1024]{1,0:T(8,128)(2,1)} all-reduce(f32[128,1024]{1,0:T(8,128)S(1)} %bitcast_convert_fusion), channel_id=1, replica_groups=mesh['dp'=64,'shard'=8] {'dp'}, use_global_device_ids=true, to_apply=%region_0.0 | all-reduce | flops 131072 | bytes 786432 | tf_op jit(solution)/shard_map/psum | solution.py:33
  572.1 0.7 convert_element_type.86
  572.9 69.5 %all-gather.12.cloned.1.call-done = bf16[1024,1024]{1,0:T(8,128)(2,1)} async-done(((bf16[128,1024]{1,0:T(8,128)(2,1)}), bf16[1024,1024]{1,0:T(8,128)(2,1)}) %all-gather.12.cloned.1.call-update) | async-done | bytes 2097168 | tf_op jit(solution)/shard_map/all_gather | solution.py:35
  642.4 3.6 multiply_reduce_fusion.1
  646.0 65.7 %all-gather.8.cloned.1.call-done = bf16[1024,1024]{1,0:T(8,128)(2,1)} async-done(((bf16[128,1024]{1,0:T(8,128)(2,1)}), bf16[1024,1024]{1,0:T(8,128)(2,1)}) %all-gather.8.cloned.1.call-update) | async-done | bytes 2097168 | tf_op jit(solution)/shard_map/all_gather | solution.py:44
  711.8 2.6 multiply_reduce_fusion
  714.4 27.4 %all-reduce = (f32[1024]{0:T(1024)S(1)}, f32[1024]{0:T(1024)S(1)}) all-reduce(f32[1024]{0:T(1024)S(1)} %get-tuple-element.16, f32[1024]{0:T(1024)S(1)} %get-tuple-element.18), channel_id=1, replica_groups=mesh['dp'=64,'shard'=8] {'shard'}, use_global_device_ids=true, to_apply=%region_2.0 | all-reduce | flops 2048 | bytes 16384 | tf_op jit(solution)/shard_map/psum | solution.py:69
  741.9 0.8 divide_convert_fusion.1
  742.7 0.8 divide_convert_fusion
  743.6 70.2 %all-gather.14.cloned.1.call-done = bf16[1024,1024]{1,0:T(8,128)(2,1)} async-done(((bf16[128,1024]{1,0:T(8,128)(2,1)}), bf16[1024,1024]{1,0:T(8,128)(2,1)}) %all-gather.14.cloned.1.call-update) | async-done | bytes 2097168 | tf_op jit(solution)/shard_map/all_gather | solution.py:84
  813.7 4.1 fusion.10
  818.4 0.8 copy.25
  819.1 6.7 all-to-all-start.1
  825.9 57.3 %all-gather.18.cloned.1.call-done = bf16[1024,1024]{1,0:T(8,128)(2,1)} async-done(((bf16[128,1024]{1,0:T(8,128)(2,1)}), bf16[1024,1024]{1,0:T(8,128)(2,1)}) %all-gather.18.cloned.1.call-update) | async-done | bytes 2097168 | tf_op jit(solution)/shard_map/all_gather | solution.py:85
  883.3 4.1 fusion.12
  887.8 0.8 copy.26
  888.6 6.3 all-to-all-start
  894.9 1.2 copy.14
  896.1 3.0 bitcast_add_fusion
  899.1 7.8 all-to-all-done
  906.8 4.4 fusion.20
  911.3 1.7 copy.24
  913.0 11.0 %all-to-all-start.2 = ((bf16[8,128,128]{1,2,0:T(8,128)(2,1)}), bf16[8,128,128]{1,2,0:T(8,128)(2,1)S(1)}, u32[]{:S(2)}, u32[]{:S(2)}) async-start(bf16[8,128,128]{1,2,0:T(8,128)(2,1)} %bitcast.65), calls=%async_computation.2 | async-start | bytes 524288 | tf_op jit(solution)/shard_map/all_to_all | solution.py:61
  924.0 1.0 copy.17
  925.0 20.1 %all-to-all-done.2 = bf16[8,128,128]{1,2,0:T(8,128)(2,1)S(1)} async-done(((bf16[8,128,128]{1,2,0:T(8,128)(2,1)}), bf16[8,128,128]{1,2,0:T(8,128)(2,1)S(1)}, u32[]{:S(2)}, u32[]{:S(2)}) %all-to-all-start.2) | async-done | bytes 262176 | tf_op jit(solution)/shard_map/all_to_all | solution.py:61
  945.1 1.5 fusion.13
  946.7 14.8 %all-gather.16.cloned.1.call-done = bf16[1024,1024]{1,0:T(8,128)(2,1)} async-done(((bf16[128,1024]{1,0:T(8,128)(2,1)}), bf16[1024,1024]{1,0:T(8,128)(2,1)}) %all-gather.16.cloned.1.call-update) | async-done | bytes 2097168 | tf_op jit(solution)/shard_map/all_gather | solution.py:84
  961.4 4.2 fusion.3
  965.6 62.9 %all-gather.20.cloned.1.call-done = bf16[1024,1024]{1,0:T(8,128)(2,1)} async-done(((bf16[128,1024]{1,0:T(8,128)(2,1)}), bf16[1024,1024]{1,0:T(8,128)(2,1)}) %all-gather.20.cloned.1.call-update) | async-done | bytes 2097168 | tf_op jit(solution)/shard_map/all_gather | solution.py:85
  1028.4 4.2 fusion
  (40 shorter events, 1.4 us)
Async XLA Ops:
  7.2 564.9 %copy-start.8 = (f32[128,1024]{1,0:T(8,128)S(1)}, f32[128,1024]{1,0:T(8,128)}, u32[]{:S(2)}) copy-start(f32[128,1024]{1,0:T(8,128)} %param.13) | copy-start | bytes 1572868
  7.2 635.2 %copy-start.7 = (f32[128,1024]{1,0:T(8,128)S(1)}, f32[128,1024]{1,0:T(8,128)}, u32[]{:S(2)}) copy-start(f32[128,1024]{1,0:T(8,128)} %param.10) | copy-start | bytes 1572868
  7.2 565.7 %all-gather.10.cloned.1.call-start = ((), (), s32[]{:S(2)}) async-start(), calls=%async_computation.4 | async-start | bytes 2359296 | tf_op jit(solution)/shard_map/all_gather | solution.py:43
  9.1 633.3 %all-gather.12.cloned.1.call-start = ((), (), s32[]{:S(2)}) async-start(), calls=%async_computation.5 | async-start | bytes 2359296 | tf_op jit(solution)/shard_map/all_gather | solution.py:35
  572.0 139.7 %all-gather.8.cloned.1.call-start = ((), (), s32[]{:S(2)}) async-start(), calls=%async_computation.3 | async-start | bytes 2359296 | tf_op jit(solution)/shard_map/all_gather | solution.py:44
  572.8 240.9 %all-gather.14.cloned.1.call-start = ((), (), s32[]{:S(2)}) async-start(), calls=%async_computation.6 | async-start | bytes 2359296 | tf_op jit(solution)/shard_map/all_gather | solution.py:84
  642.4 69.4 %copy-start.1 = (bf16[1024,1024]{1,0:T(8,128)(2,1)S(1)}, bf16[1024,1024]{1,0:T(8,128)(2,1)}, u32[]{:S(2)}) copy-start(bf16[1024,1024]{1,0:T(8,128)(2,1)} %all-gather.12.cloned.1.call-done) | copy-start | bytes 6291460
  742.7 140.6 %all-gather.18.cloned.1.call-start = ((), (), s32[]{:S(2)}) async-start(), calls=%async_computation.8 | async-start | bytes 2359296 | tf_op jit(solution)/shard_map/all_gather | solution.py:85
  743.5 74.4 %copy-start = (bf16[1024,1024]{1,0:T(8,128)(2,1)S(1)}, bf16[1024,1024]{1,0:T(8,128)(2,1)}, u32[]{:S(2)}) copy-start(bf16[1024,1024]{1,0:T(8,128)(2,1)} %all-gather.8.cloned.1.call-done) | copy-start | bytes 6291460
  743.5 74.4 %copy-start.2 = (bf16[128,1024]{1,0:T(8,128)(2,1)S(1)}, bf16[128,1024]{1,0:T(8,128)(2,1)}, u32[]{:S(2)}) copy-start(bf16[128,1024]{1,0:T(8,128)(2,1)} %all-reduce.2) | copy-start | bytes 786436
  743.5 217.9 %all-gather.16.cloned.1.call-start = ((), (), s32[]{:S(2)}) async-start(), calls=%async_computation.7 | async-start | bytes 2359296 | tf_op jit(solution)/shard_map/all_gather | solution.py:84
  817.9 65.4 %copy-start.5 = (bf16[128,1024]{1,0:T(8,128)(2,1)S(1)}, bf16[128,1024]{1,0:T(8,128)(2,1)}, u32[]{:S(2)}) copy-start(bf16[128,1024]{1,0:T(8,128)(2,1)} %divide_convert_fusion) | copy-start | bytes 786436
  819.1 69.5 %all-to-all-start.1 = ((bf16[128,8,128]{2,0,1:T(8,128)(2,1)}), bf16[128,8,128]{2,0,1:T(8,128)(2,1)S(1)}, u32[]{:S(2)}, u32[]{:S(2)}) async-start(bf16[128,8,128]{2,0,1:T(8,128)(2,1)} %bitcast.66), calls=%async_computation.1 | async-start | bytes 524288 | tf_op jit(solution)/shard_map/all_to_all | solution.py:53
  825.9 61.5 %copy-start.9 = (f32[128,1024]{1,0:T(8,128)S(1)}, f32[128,1024]{1,0:T(8,128)}, u32[]{:S(2)}) copy-start(f32[128,1024]{1,0:T(8,128)} %param.8) | copy-start | bytes 1572868
  825.9 202.6 %all-gather.20.cloned.1.call-start = ((), (), s32[]{:S(2)}) async-start(), calls=%async_computation.9 | async-start | bytes 2359296 | tf_op jit(solution)/shard_map/all_gather | solution.py:85
  888.6 7.5 copy-start.6
  888.6 18.3 %all-to-all-start = ((bf16[128,8,128]{2,0,1:T(8,128)(2,1)}), bf16[128,8,128]{2,0,1:T(8,128)(2,1)S(1)}, u32[]{:S(2)}, u32[]{:S(2)}) async-start(bf16[128,8,128]{2,0,1:T(8,128)(2,1)} %bitcast.67), calls=%async_computation | async-start | bytes 524288 | tf_op jit(solution)/shard_map/all_to_all | solution.py:54
  913.0 48.4 %copy-start.3 = (bf16[128,1024]{1,0:T(8,128)(2,1)S(1)}, bf16[128,1024]{1,0:T(8,128)(2,1)}, u32[]{:S(2)}) copy-start(bf16[128,1024]{1,0:T(8,128)(2,1)} %fusion.10) | copy-start | bytes 786436
  913.0 32.1 %all-to-all-start.2 = ((bf16[8,128,128]{1,2,0:T(8,128)(2,1)}), bf16[8,128,128]{1,2,0:T(8,128)(2,1)S(1)}, u32[]{:S(2)}, u32[]{:S(2)}) async-start(bf16[8,128,128]{1,2,0:T(8,128)(2,1)} %bitcast.65), calls=%async_computation.2 | async-start | bytes 524288 | tf_op jit(solution)/shard_map/all_to_all | solution.py:61
  946.7 81.8 %copy-start.4 = (bf16[128,1024]{1,0:T(8,128)(2,1)S(1)}, bf16[128,1024]{1,0:T(8,128)(2,1)}, u32[]{:S(2)}) copy-start(bf16[128,1024]{1,0:T(8,128)(2,1)} %fusion.12) | copy-start | bytes 786436
Sparse Core Ops, SparseCore 0:
  10.7 73.9 all-gather.9
  572.1 70.2 all-gather.11
  645.1 66.6 all-gather.7
  742.8 70.9 all-gather.13
  816.2 66.9 all-gather.17
  885.2 76.1 all-gather.15
  963.5 64.9 all-gather.19
where the time goes:
time: 1040 us
  blocking collectives  589 us (57%)
  waiting for transfers between devices  368 us (35%)
  matrix products  32.6 us (3%)
  starting transfers between devices  24.3 us (2%)
  between operations  14.3 us (1%)
    psum x1, blocking collectives, body(): summed = lax.psum(local_sum, 'dp')  562 us
    all_gather x2, waiting for transfers between devices, body(): lax.all_gather(right_current, 'shard', axis=0, tiled=True)  120 us
    all_gather x2, waiting for transfers between devices, body(): lax.all_gather(left_current, 'shard', axis=0, tiled=True)  84.9 us
    all_gather x1, waiting for transfers between devices, body(): gradient = lax.all_gather(grad_rows, 'shard', axis=0, tiled=True)  69.5 us
    all_gather x1, waiting for transfers between devices, body(): lax.all_gather(basis_right.astype(jnp.bfloat16), 'shard', axis=0, tiled=T...  65.7 us
    psum x1, blocking collectives, body(): lax.psum((jnp.sum(left_product * left_product, axis=0), jnp.sum(right_pro...  27.4 us
  transfers between devices with their start and end apart: 10, of which 8 were waited for; matrix products, arithmetic and copies ran while one was open for 3% of the time, Pallas kernels for 0%

commit v1 on v0

v1 whole, which is shorter than its diff:
```python
import jax
import jax.numpy as jnp
from jax import lax
from jax.experimental import pallas as pl
from jax.experimental.pallas import tpu as pltpu
from jax.sharding import PartitionSpec as P

NS_ITERS = 2


BETA_ONE = 0.9
BETA_TWO = 0.9
BETA_STAT = 0.95
EPSILON = 1e-08
NORM_EPS = 1e-06

ORDER = 1024
SHARDS = 8
ROWS = ORDER // SHARDS
SIDE = 4
COLS = ORDER // SIDE
COPIES = 100
LOCALS = 5


def contract_rows(left_mat, right_mat):
    return lax.dot_general(
        left_mat, right_mat, (((0,), (0,)), ((), ())), preferred_element_type=jnp.float32
    )


def contract_cols(left_mat, right_mat):
    return lax.dot_general(
        left_mat, right_mat, (((1,), (1,)), ((), ())), preferred_element_type=jnp.float32
    )


class Place:
    def __init__(self):
        data = lax.axis_index("dp")
        self.z = lax.axis_index("shard")
        self.core = lax.rem(data, 2)
        self.zhi = lax.rem(lax.div(data, 2), 2)
        y = lax.rem(lax.div(data, 4), 4)
        x = lax.div(data, 16)
        self.p = x + self.core * (y - x)
        self.q = y + self.core * (x - y)

    def at(self, p, q, zhi, core):
        x = p + self.core * (q - p)
        y = q + self.core * (p - q)
        return ((x * 4 + y) * 2 + zhi) * 2 + core

    def along_p(self, step):
        p = lax.rem(self.p + step, SIDE)
        return (self.at(p, self.q, self.zhi, self.core), self.z)

    def along_q(self, step):
        q = lax.rem(self.q + step, SIDE)
        return (self.at(self.p, q, self.zhi, self.core), self.z)

    def along_z(self, step):
        z = lax.rem(self.z + step, SHARDS)
        return (self.at(self.p, self.q, self.zhi, self.core), z)

    def far(self):
        return (self.at(self.p, self.q, 1 - self.zhi, self.core), self.z)

    def sibling(self):
        return (self.at(self.p, self.q, self.zhi, 1 - self.core), self.z)


class Copies:
    def __init__(self, send, recv):
        self.send, self.recv, self.count, self.started = send, recv, 0, []

    def start(self, src, dst, device):
        copy = pltpu.make_async_remote_copy(
            src_ref=src,
            dst_ref=dst,
            send_sem=self.send.at[self.count],
            recv_sem=self.recv.at[self.count],
            device_id=device,
            device_id_type=pl.DeviceIdType.MESH,
        )
        self.count += 1
        copy.start()
        self.started.append(copy)
        return copy

    def finish(self):
        for copy in self.started:
            copy.wait_send()


class Gather:
    def __init__(self, place, copies, local_sem, out, both):
        self.place, self.copies, self.local_sem = place, copies, local_sem
        self.out, self.both = out, both
        self.height = ROWS // SIDE // (2 if both else 1)
        self.base = place.core * (ROWS // 2) if both else 0
        self.to_core = []

    def rows(self, p):
        return pl.ds(pl.multiple_of(self.base + p * self.height, self.height), self.height)

    def cols(self, q):
        return pl.ds(pl.multiple_of(q * COLS, COLS), COLS)

    def piece(self, ref):
        return ref.at[self.rows(self.place.p), self.cols(self.place.q)]

    def z_stage(self, piece):
        place = self.place
        spot = self.out.at[place.z, self.rows(place.p), self.cols(place.q)]
        self.local = pltpu.make_async_copy(piece, spot, self.local_sem)
        self.local.start()
        self.stage = [
            self.copies.start(piece, spot, place.along_z(step)) for step in (7, 1, 6, 2, 5, 3, 4)
        ]

    def arrived(self):
        for copy in self.stage:
            copy.wait_recv()

    def q_spot(self, step, zs):
        q = lax.rem(self.place.q + step, SIDE)
        return self.out.at[zs, self.rows(self.place.p), self.cols(q)]

    def p_spot(self, step, zs):
        p = lax.rem(self.place.p + step, SIDE)
        return self.out.at[zs, self.rows(p), :]

    def q_first(self):
        self.local.wait()
        self.arrived()
        self.ring_first(self.q_spot, self.place.along_q)

    def q_second(self):
        self.arrived()
        self.ring_second(self.q_spot, self.place.along_q)

    def p_first(self):
        self.arrived()
        self.ring_first(self.p_spot, self.place.along_p)
        self.share(0)

    def p_second(self):
        self.arrived()
        self.ring_second(self.p_spot, self.place.along_p)
        self.share(1)
        self.share(3)

    def p_third(self):
        self.arrived()
        self.share(2)

    def finish(self):
        for copy in self.to_core:
            copy.wait_recv()

    def ring_first(self, spot, along):
        whole = pl.ds(0, SHARDS)
        own = spot(0, whole)
        self.stage = [
            self.copies.start(own, own, along(1)),
            self.copies.start(own, own, along(3)),
        ]

    def ring_second(self, spot, along):
        low, high = pl.ds(0, SHARDS // 2), pl.ds(SHARDS // 2, SHARDS // 2)
        self.stage = [
            self.copies.start(spot(3, low), spot(3, low), along(1)),
            self.copies.start(spot(1, high), spot(1, high), along(3)),
        ]

    def share(self, step):
        if self.both:
            block = self.p_spot(step, pl.ds(0, SHARDS))
            self.to_core.append(self.copies.start(block, block, self.place.sibling()))


def collect_kernel(
    grads, moment, stat, base_left, base_right,
    out_grad, out_moment, out_left, out_right, out_stat,
    recv0, acc0, recv1, acc1, recv2, acc2, recv3, grad_piece, moment_piece,
    send, recv, local,
):
    place = Place()
    barrier = pltpu.get_barrier_semaphore()
    partners = [place.sibling(), place.far()]
    partners += [place.along_p(step) for step in (1, 2, 3)]
    partners += [place.along_q(step) for step in (1, 2, 3)]
    partners += [place.along_z(step) for step in range(1, SHARDS)]
    for partner in partners:
        pl.semaphore_signal(
            barrier, inc=1, device_id=partner, device_id_type=pl.DeviceIdType.MESH
        )
    pl.semaphore_wait(barrier, len(partners))

    copies = Copies(send, recv)
    half = ROWS // 2
    mine = pl.ds(pl.multiple_of(place.core * half, half), half)
    theirs = pl.ds(pl.multiple_of((1 - place.core) * half, half), half)
    g, m, l, r, s = [
        Gather(place, copies, local.at[index], out, both)
        for index, (out, both) in enumerate(
            (
                (out_grad, True),
                (out_moment, True),
                (out_left, True),
                (out_right, True),
                (out_stat, False),
            )
        )
    ]

    core_copy = copies.start(grads.at[theirs, :], recv0, place.sibling())
    l.z_stage(l.piece(base_left))
    r.z_stage(r.piece(base_right))
    s.z_stage(s.piece(stat))

    core_copy.wait_recv()
    acc0[...] = (
        grads[mine, :].astype(jnp.float32) + recv0[...].astype(jnp.float32)
    ).reshape(acc0.shape)
    p_copies = [
        copies.start(
            acc0.at[lax.rem(place.p + step, SIDE)], recv1.at[step - 1], place.along_p(step)
        )
        for step in (1, 3, 2)
    ]
    for copy in p_copies:
        copy.wait_recv()
    acc1[...] = (acc0[place.p] + recv1[0]) + (recv1[1] + recv1[2])
    q_copies = [
        copies.start(
            acc1.at[:, g.cols(lax.rem(place.q + step, SIDE))],
            recv2.at[step - 1],
            place.along_q(step),
        )
        for step in (1, 3, 2)
    ]
    for copy in q_copies:
        copy.wait_recv()
    acc2[...] = (acc1[:, g.cols(place.q)] + recv2[0]) + (recv2[1] + recv2[2])
    far_copy = copies.start(acc2, recv3, place.far())
    l.q_first()
    r.q_first()
    far_copy.wait_recv()
    piece = (acc2[...] + recv3[...]).astype(jnp.bfloat16)
    grad_piece[...] = piece
    old = moment[g.rows(place.p), g.cols(place.q)]
    moment_piece[...] = (
        BETA_ONE * old + (1.0 - BETA_ONE) * piece.astype(jnp.float32)
    ).astype(jnp.bfloat16)
    g.z_stage(grad_piece)
    m.z_stage(moment_piece)

    l.q_second()
    r.q_second()
    s.q_first()
    l.p_first()
    r.p_first()
    s.q_second()
    g.q_first()
    m.q_first()
    s.p_first()
    g.q_second()
    m.q_second()
    l.p_second()
    r.p_second()
    g.p_first()
    m.p_first()
    l.p_third()
    r.p_third()
    s.p_second()
    g.p_second()
    m.p_second()
    g.p_third()
    m.p_third()
    s.p_third()
    for gather in (l, r, g, m):
        gather.finish()
    copies.finish()


def collect(grads, moment, stat, base_left, base_right):
    whole = (SHARDS, ROWS, ORDER)
    vmem = pl.BlockSpec(memory_space=pltpu.VMEM)
    outs = [jax.ShapeDtypeStruct(whole, jnp.bfloat16)] * 4
    outs += [jax.ShapeDtypeStruct(whole, jnp.float32)]
    height = ROWS // SIDE // 2
    f32, bf16 = jnp.float32, jnp.bfloat16
    return pl.pallas_call(
        collect_kernel,
        out_shape=outs,
        in_specs=[vmem] * 5,
        out_specs=[vmem] * 5,
        scratch_shapes=[
            pltpu.VMEM((ROWS // 2, ORDER), bf16),
            pltpu.VMEM((SIDE, height, ORDER), f32),
            pltpu.VMEM((SIDE - 1, height, ORDER), f32),
            pltpu.VMEM((height, ORDER), f32),
            pltpu.VMEM((SIDE - 1, height, COLS), f32),
            pltpu.VMEM((height, COLS), f32),
            pltpu.VMEM((height, COLS), f32),
            pltpu.VMEM((height, COLS), bf16),
            pltpu.VMEM((height, COLS), bf16),
            pltpu.SemaphoreType.DMA((COPIES,)),
            pltpu.SemaphoreType.DMA((COPIES,)),
            pltpu.SemaphoreType.DMA((LOCALS,)),
        ],
        compiler_params=pltpu.CompilerParams(collective_id=0, has_side_effects=True),
        name="collect",
    )(grads, moment, stat, base_left, base_right)


def body(group_grads, moment, second, stat_left, stat_right, basis_left, basis_right):
    position = lax.axis_index("shard")
    core = lax.rem(lax.axis_index("dp"), 2)
    is_left = core == 0
    row_start = position * ROWS
    gradient, moment_half, left_rot, right_rot, stat = collect(
        group_grads[0],
        moment,
        jnp.where(is_left, stat_left, stat_right),
        basis_left.astype(jnp.bfloat16),
        basis_right.astype(jnp.bfloat16),
    )
    gradient, moment_half, left_rot, right_rot, stat = [
        array.reshape(ORDER, ORDER)
        for array in (gradient, moment_half, left_rot, right_rot, stat)
    ]

    right_cols = lax.dynamic_slice_in_dim(right_rot, row_start, ROWS, 1)
    grad_block = jnp.dot(gradient, right_cols, preferred_element_type=jnp.float32).astype(
        jnp.bfloat16
    )
    moment_block = jnp.dot(moment_half, right_cols, preferred_element_type=jnp.float32).astype(
        jnp.bfloat16
    )
    grad_rot = contract_rows(left_rot, grad_block) / ORDER
    moment_rot = contract_rows(left_rot, moment_block) / ORDER
    second_new = BETA_TWO * second + (1.0 - BETA_TWO) * grad_rot * grad_rot
    scaled = (moment_rot / (jnp.sqrt(second_new) + EPSILON)).astype(jnp.bfloat16)
    turned_back = jnp.dot(left_rot, scaled, preferred_element_type=jnp.float32).astype(jnp.bfloat16)
    back_rows = lax.all_to_all(turned_back, "shard", split_axis=0, concat_axis=1, tiled=True)
    update = (contract_cols(back_rows, right_rot) / ORDER).astype(jnp.bfloat16)

    outer = lax.cond(
        is_left,
        lambda g: contract_cols(g, g),
        lambda g: contract_rows(g, g),
        gradient,
    )
    stat_new = (BETA_STAT * stat + (1.0 - BETA_STAT) * outer).astype(jnp.bfloat16)
    rot = jnp.where(is_left, left_rot, right_rot)
    product = jnp.dot(stat_new, rot, preferred_element_type=jnp.float32)
    squares = jnp.sum(product * product, axis=0)
    current = (product / jnp.sqrt(squares / ORDER + NORM_EPS)).astype(jnp.bfloat16)
    for _ in range(NS_ITERS - 1):
        gram = (contract_cols(current, current) / ORDER).astype(jnp.bfloat16)
        current = (
            1.5 * current.astype(jnp.float32)
            - 0.5 * jnp.dot(gram, current, preferred_element_type=jnp.float32)
        ).astype(jnp.bfloat16)
    rows = lax.dynamic_slice_in_dim(current, row_start, ROWS, 0)
    gram = (contract_cols(rows, current) / ORDER).astype(jnp.bfloat16)
    result = 1.5 * rows.astype(jnp.float32) - 0.5 * jnp.dot(
        gram, current, preferred_element_type=jnp.float32
    )
    size = lax.axis_size("dp")
    other = lax.ppermute(result, "dp", [(i, i ^ 1) for i in range(size)])
    left_result = jnp.where(is_left, result, other)
    right_result = jnp.where(is_left, other, result)
    return (update, second_new, left_result, right_result)


def solution(mesh):
    return jax.shard_map(
        body,
        mesh=mesh,
        in_specs=(
            P("dp", "shard", None),
            P("shard", None),
            P(None, "shard"),
            P("shard", None),
            P("shard", None),
            P("shard", None),
            P("shard", None),
        ),
        out_specs=(P("shard", None), P(None, "shard"), P("shard", None), P("shard", None)),
        check_vma=False,
    )
```

time: 1040 us -> 154 us (0.15)
  blocking collectives: 589 us -> 0 us
  waiting for transfers between devices: 368 us -> 1.65 us
  Pallas kernels: 0 us -> 96.7 us
  starting transfers between devices: 24.3 us -> 8.75 us
  between operations: 14.3 us -> 0.76 us
    psum x2 -> x0, blocking collectives: 589 us -> none  [the longest x1 562 us: body(): summed = lax.psum(local_sum, 'dp')]
    all_gather x7 -> x0, waiting for transfers between devices: 340 us -> none  [the longest x2 120 us: body(): lax.all_gather(right_current, 'shard', axis=0, tiled=True)]
    pallas_call x0 -> x1, Pallas kernels: none -> 96.7 us  [collect(): pl.pallas_call(collect_kernel, out_shape=outs, in_specs=[vmem] * 5, out_s...]
    all_to_all x1, waiting for transfers between devices: 20.1 us -> 0.01 us  [body(): lax.all_to_all(turned_back, 'shard', split_axis=0, concat_axis=1, tiled=T...]
    all_to_all x2 -> x0, starting transfers between devices: 13 us -> none  [the longest x1 6.74 us: body(): lax.all_to_all(grad_turned, 'shard', split_axis=1, concat_axis=0, tiled=T...]
    dot_general x1 -> x3, matrix products: 2.98 us -> 15.2 us  [contract_rows(): lax.dot_general(left_mat, right_mat, (((0,), (0,)), ((), ())), preferred_...]
    dot_general x8 -> x3, matrix products: 23.7 us -> 16.1 us  [the longest x2 11.8 us: body(): jnp.dot(gram, current, preferred_element_type=jnp.float32)]
  transfers between devices with their start and end apart: 10 -> 2, of which waited for: 8 -> 1; matrix products, arithmetic and copies ran while one was open for 3% -> 18% of each run, Pallas kernels for 0% -> 0%
where the time goes in v1:
time: 154 us
  Pallas kernels  96.7 us (63%)
  matrix products  33.5 us (22%)
  other arithmetic  10.6 us (7%)
  starting transfers between devices  8.75 us (6%)
  local copies, waits for them, and re-layouts  1.92 us (1%)
  waiting for transfers between devices  1.65 us (1%)
    pallas_call x1, Pallas kernels, collect(): pl.pallas_call(collect_kernel, out_shape=outs, in_specs=[vmem] * 5, out_s...  96.7 us
    dot_general x3, matrix products, contract_rows(): lax.dot_general(left_mat, right_mat, (((0,), (0,)), ((), ())), preferred_...  15.2 us
    dot_general x2, matrix products, body(): jnp.dot(gram, current, preferred_element_type=jnp.float32)  11.8 us
    all_to_all x1, starting transfers between devices, body(): lax.all_to_all(turned_back, 'shard', split_axis=0, concat_axis=1, tiled=T...  6.46 us
    dot_general x1, matrix products, body(): product = jnp.dot(stat_new, rot, preferred_element_type=jnp.float32)  4.3 us
  transfers between devices with their start and end apart: 2, of which 1 were waited for; matrix products, arithmetic and copies ran while one was open for 18% of the time, Pallas kernels for 0%

profile of v1, /device:TPU:1, one launch (start us, length us, event | category | flops | bytes accessed | tf_op | source)
XLA Modules:
  0.0 153.8 jit_solution(10177135797328328874)
XLA Ops:
  0.6 1.8 %convert_element_type.45.base_left = bf16[128,1024]{1,0:T(8,128)(2,1)} convert(f32[128,1024]{1,0:T(8,128)} %param.14) | non-fusion elementwise | flops 131072 | bytes 786432 | tf_op jit(solution)/shard_map/convert_element_type | solution.py:328
  2.4 0.0 copy-start.4
  2.4 1.8 %convert_element_type.46.base_right = bf16[128,1024]{1,0:T(8,128)(2,1)} convert(f32[128,1024]{1,0:T(8,128)} %param.15) | non-fusion elementwise | flops 131072 | bytes 786432 | tf_op jit(solution)/shard_map/convert_element_type | solution.py:329
  4.3 1.9 %broadcast_select_fusion.2.stat = f32[128,1024]{1,0:T(8,128)} fusion(f32[128,1024]{1,0:T(8,128)} %param.12, f32[128,1024]{1,0:T(8,128)} %param.13, pred[]{:T(512)S(6)} %eq.3), kind=kLoop, calls=%fused_computation.28 | loop fusion | flops 131072 | bytes 1572865 | tf_op jit(solution)/shard_map/jit(_where)/select_n | solution.py:327
  6.2 96.7 %collect.1 = (bf16[8,128,1024]{2,1,0:T(8,128)(2,1)}, bf16[8,128,1024]{2,1,0:T(8,128)(2,1)}, bf16[8,128,1024]{2,1,0:T(8,128)(2,1)}, bf16[8,128,1024]{2,1,0:T(8,128)(2,1)}, f32[8,128,1024]{2,1,0:T(8,128)}) custom-call(bf16[128,1024]{1,0:T(8,128)(2,1)} %bitcast.41, f32[128,1024]{1,0:T(8,128)} %moment.1, f32[128,1024]{1,0:T(8,128)} %broadcast_select_fusion.2.stat, ...), custom_call_target="tpu_custom_call" | custom-call | tf_op jit(solution)/shard_map/collect/pallas_call | solution.py:295
  102.8 0.0 copy-done.4
  102.9 0.0 copy-start
  102.9 4.6 %multiply_add_fusion = f32[1024,128]{1,0:T(8,128)S(1)} fusion(bf16[1024,1024]{1,0:T(8,128)(2,1)} %bitcast.28, bf16[1024,1024]{1,0:T(8,128)(2,1)} %bitcast.36, f32[1024,128]{1,0:T(8,128)S(1)} %copy-done.4, bf16[1024,1024]{1,0:T(8,128)(2,1)} %bitcast.32, s32[]{:T(128)S(6)} %select_n.30), kind=kOutput, calls=%fused_computation.23 | convolution fusion | flops 537657344 | bytes 5505028 | tf_op jit(solution)/shard_map/dot_general | solution.py:27
  107.5 0.0 copy-start.5
  107.5 0.0 copy-done
  107.5 4.0 %fusion.6 = bf16[1024,128]{1,0:T(8,128)(2,1)S(1)} fusion(bf16[1024,1024]{1,0:T(8,128)(2,1)S(1)} %bitcast.29, bf16[1024,1024]{1,0:T(8,128)(2,1)} %bitcast.42, f32[1024,128]{1,0:T(8,128)S(1)} %multiply_add_fusion, bf16[1024,1024]{1,0:T(8,128)(2,1)} %bitcast.33, s32[]{:T(128)S(6)} %select_n.30), kind=kOutput, calls=%fused_computation.16 | convolution fusion | flops 537526272 | bytes 5242884 | tf_op jit(solution)/shard_map/dot_general | solution.py:27
  111.5 0.0 copy-done.5
  111.5 0.7 convolution_convert_fusion
  112.2 0.9 copy.11
  113.1 6.5 %all-to-all-start = ((bf16[8,128,128]{1,2,0:T(8,128)(2,1)}), bf16[8,128,128]{1,2,0:T(8,128)(2,1)S(1)}, u32[]{:S(2)}, u32[]{:S(2)}) async-start(bf16[8,128,128]{1,2,0:T(8,128)(2,1)} %copy.11), calls=%async_computation | async-start | bytes 524288 | tf_op jit(solution)/shard_map/all_to_all | solution.py:348
  119.5 6.6 %conditional.1 = (f32[1024,1024]{1,0:T(8,128)}) conditional(s32[]{:T(128)} %convert_element_type.52, bf16[1024,1024]{1,0:T(8,128)(2,1)} %bitcast.37, bf16[1024,1024]{1,0:T(8,128)(2,1)} %bitcast.38), branch_computations={%region_0.1_spmd, %region_1.2_spmd} | conditional | flops 2147483648 | bytes 6291464 | solution.py:351
  119.5 6.6 %fusion.25 = f32[1024,1024]{1,0:T(8,128)} fusion(bf16[1024,1024]{1,0:T(8,128)(2,1)} %param), kind=kOutput, calls=%fused_computation.37 | convolution fusion | flops 2147483648 | bytes 6291456 | tf_op jit(solution)/shard_map/cond/branch_0_fun/dot_general | solution.py:27
  126.1 0.0 copy-start.1
  126.1 2.8 %broadcast_multiply_fusion = f32[8,128,1024]{2,1,0:T(8,128)S(1)} fusion(f32[8,128,1024]{2,1,0:T(8,128)} %get-tuple-element.18), kind=kLoop, calls=%fused_computation.8 | loop fusion | flops 1048576 | bytes 8388608 | tf_op jit(solution)/shard_map/mul | solution.py:357
  129.0 0.6 copy-done.1
  129.6 1.1 fusion
  130.7 0.4 copy-done.2
  131.1 4.3 %multiply_reduce_fusion = (f32[1024]{0:T(1024)S(1)}, f32[1024,1024]{1,0:T(8,128)}) fusion(bf16[1024,1024]{1,0:T(8,128)(2,1)S(1)} %fusion, bf16[1024,1024]{1,0:T(8,128)(2,1)S(1)} %bitcast.31, bf16[1024,1024]{1,0:T(8,128)(2,1)S(1)} %bitcast.34, pred[]{:T(512)S(6)} %eq.3), kind=kOutput, calls=%fused_computation.5 | convolution fusion | flops 2150628352 | bytes 10489857 | tf_op jit(solution)/shard_map/dot_general | solution.py:359
  135.5 10.6 %subtract_convert_fusion = bf16[1024,1024]{1,0:T(8,128)(2,1)S(1)} fusion(f32[1024,1024]{1,0:T(8,128)} %get-tuple-element.22, f32[1024]{0:T(1024)S(1)} %add_sqrt_fusion), kind=kOutput, calls=%fused_computation.2 | convolution fusion | flops 4308598784 | bytes 6295552 | tf_op jit(solution)/shard_map/dot_general | solution.py:366
  146.1 1.1 fusion.4
  147.2 0.0 copy-start.3
  147.3 2.3 %collective-permute-start = (f32[128,1024]{1,0:T(8,128)S(1)}, f32[128,1024]{1,0:T(8,128)S(1)}, u32[]{:S(2)}, u32[]{:S(2)}) collective-permute-start(f32[128,1024]{1,0:T(8,128)S(1)} %fusion.4), channel_id=1, source_target_pairs={{0,8},{8,0},{16,24},{24,16},{32,40},{40,32},{48,56},{56,48},{64,72... | collective-permute-start | bytes 1572872 | tf_op jit(solution)/shard_map/ppermute | solution.py:374
  149.5 1.6 %collective-permute-done = f32[128,1024]{1,0:T(8,128)S(1)} collective-permute-done((f32[128,1024]{1,0:T(8,128)S(1)}, f32[128,1024]{1,0:T(8,128)S(1)}, u32[]{:S(2)}, u32[]{:S(2)}) %collective-permute-start) | collective-permute-done | bytes 524320 | tf_op jit(solution)/shard_map/ppermute | solution.py:374
  151.2 1.1 broadcast_select_fusion
  152.3 0.0 all-to-all-done
  152.3 0.0 copy-done.3
  152.3 1.5 fusion.7
  (2 shorter events, 0.0 us)
Async XLA Ops:
  2.4 100.4 %copy-start.4 = (f32[1024,128]{1,0:T(8,128)S(1)}, f32[1024,128]{1,0:T(8,128)}, u32[]{:S(2)}) copy-start(f32[1024,128]{1,0:T(8,128)} %param.11) | copy-start | bytes 1572868
  102.9 4.6 %copy-start = (bf16[8,128,1024]{2,1,0:T(8,128)(2,1)S(1)}, bf16[8,128,1024]{2,1,0:T(8,128)(2,1)}, u32[]{:S(2)}) copy-start(bf16[8,128,1024]{2,1,0:T(8,128)(2,1)} %get-tuple-element.14) | copy-start | bytes 6291460
  107.5 4.0 %copy-start.5 = (f32[1024,128]{1,0:T(8,128)}, f32[1024,128]{1,0:T(8,128)S(1)}, u32[]{:S(2)}) copy-start(f32[1024,128]{1,0:T(8,128)S(1)} %multiply_add_fusion) | copy-start | bytes 1572868
  113.1 39.2 %all-to-all-start = ((bf16[8,128,128]{1,2,0:T(8,128)(2,1)}), bf16[8,128,128]{1,2,0:T(8,128)(2,1)S(1)}, u32[]{:S(2)}, u32[]{:S(2)}) async-start(bf16[8,128,128]{1,2,0:T(8,128)(2,1)} %copy.11), calls=%async_computation | async-start | bytes 524288 | tf_op jit(solution)/shard_map/all_to_all | solution.py:348
  126.1 3.4 %copy-start.1 = (f32[1024,1024]{1,0:T(8,128)S(1)}, f32[1024,1024]{1,0:T(8,128)}, u32[]{:S(2)}) copy-start(f32[1024,1024]{1,0:T(8,128)} %get-tuple-element.23) | copy-start | bytes 12582916
  129.6 1.6 %copy-start.2 = (bf16[8,128,1024]{2,1,0:T(8,128)(2,1)S(1)}, bf16[8,128,1024]{2,1,0:T(8,128)(2,1)}, u32[]{:S(2)}) copy-start(bf16[8,128,1024]{2,1,0:T(8,128)(2,1)} %get-tuple-element.16) | copy-start | bytes 6291460
  147.2 5.0 %copy-start.3 = (bf16[8,128,1024]{2,1,0:T(8,128)(2,1)S(1)}, bf16[8,128,1024]{2,1,0:T(8,128)(2,1)}, u32[]{:S(2)}) copy-start(bf16[8,128,1024]{2,1,0:T(8,128)(2,1)} %get-tuple-element.16) | copy-start | bytes 6291460
  147.3 3.9 %collective-permute-start = (f32[128,1024]{1,0:T(8,128)S(1)}, f32[128,1024]{1,0:T(8,128)S(1)}, u32[]{:S(2)}, u32[]{:S(2)}) collective-permute-start(f32[128,1024]{1,0:T(8,128)S(1)} %fusion.4), channel_id=1, source_target_pairs={{0,8},{8,0},{16,24},{24,16},{32,40},{40,32},{48,56},{56,48},{64,72... | collective-permute-start | bytes 1572872 | tf_op jit(solution)/shard_map/ppermute | solution.py:374

commit v2 on v1

--- a/solution.py
+++ b/solution.py
@@ -20,7 +20,7 @@
 SIDE = 4
 COLS = ORDER // SIDE
 COPIES = 100
-LOCALS = 5
+LOCALS = 6
 
 
 def contract_rows(left_mat, right_mat):
@@ -93,96 +93,138 @@
             copy.wait_send()
 
 
-class Gather:
-    def __init__(self, place, copies, local_sem, out, both):
-        self.place, self.copies, self.local_sem = place, copies, local_sem
-        self.out, self.both = out, both
-        self.height = ROWS // SIDE // (2 if both else 1)
-        self.base = place.core * (ROWS // 2) if both else 0
-        self.to_core = []
-
-    def rows(self, p):
-        return pl.ds(pl.multiple_of(self.base + p * self.height, self.height), self.height)
-
-    def cols(self, q):
-        return pl.ds(pl.multiple_of(q * COLS, COLS), COLS)
-
-    def piece(self, ref):
-        return ref.at[self.rows(self.place.p), self.cols(self.place.q)]
-
-    def z_stage(self, piece):
-        place = self.place
-        spot = self.out.at[place.z, self.rows(place.p), self.cols(place.q)]
-        self.local = pltpu.make_async_copy(piece, spot, self.local_sem)
-        self.local.start()
+class Ring:
+    def __init__(self, copies, spot, along):
+        self.copies, self.spot, self.along = copies, spot, along
+
+    def first(self):
+        own = self.spot(0, pl.ds(0, SHARDS))
         self.stage = [
-            self.copies.start(piece, spot, place.along_z(step)) for step in (7, 1, 6, 2, 5, 3, 4)
+            self.copies.start(own, own, self.along(1)),
+            self.copies.start(own, own, self.along(3)),
+        ]
+
+    def second(self):
+        self.arrived()
+        low, high = pl.ds(0, SHARDS // 2), pl.ds(SHARDS // 2, SHARDS // 2)
+        self.stage = [
+            self.copies.start(self.spot(3, low), self.spot(3, low), self.along(1)),
+            self.copies.start(self.spot(1, high), self.spot(1, high), self.along(3)),
         ]
 
     def arrived(self):
         for copy in self.stage:
             copy.wait_recv()
 
+
+class Spread:
+    def __init__(self, place, copies, piece, spot, local_sem):
+        self.local = pltpu.make_async_copy(piece, spot, local_sem)
+        self.local.start()
+        self.stage = [
+            copies.start(piece, spot, place.along_z(step)) for step in (7, 1, 6, 2, 5, 3, 4)
+        ]
+
+    def arrived(self):
+        self.local.wait()
+        for copy in self.stage:
+            copy.wait_recv()
+
+
+class Gather:
+    def __init__(self, place, copies, local_sem, out):
+        self.place, self.copies, self.local_sem, self.out = place, copies, local_sem, out
+        self.q_ring = Ring(copies, self.q_spot, place.along_q)
+        self.p_ring = Ring(copies, self.p_spot, place.along_p)
+        self.to_core = []
+
+    def rows(self, p):
+        height = ROWS // SIDE // 2
+        start = self.place.core * (ROWS // 2) + p * height
+        return pl.ds(pl.multiple_of(start, height), height)
+
+    def piece(self, ref):
+        return ref.at[self.rows(self.place.p), cols(self.place.q)]
+
+    def z_stage(self, piece):
+        place = self.place
+        spot = self.out.at[place.z, self.rows(place.p), cols(place.q)]
+        self.spread = Spread(place, self.copies, piece, spot, self.local_sem)
+
     def q_spot(self, step, zs):
         q = lax.rem(self.place.q + step, SIDE)
-        return self.out.at[zs, self.rows(self.place.p), self.cols(q)]
+        return self.out.at[zs, self.rows(self.place.p), cols(q)]
 
     def p_spot(self, step, zs):
         p = lax.rem(self.place.p + step, SIDE)
         return self.out.at[zs, self.rows(p), :]
 
     def q_first(self):
-        self.local.wait()
-        self.arrived()
-        self.ring_first(self.q_spot, self.place.along_q)
+        self.spread.arrived()
+        self.q_ring.first()
 
     def q_second(self):
-        self.arrived()
-        self.ring_second(self.q_spot, self.place.along_q)
+        self.q_ring.second()
+
+    def q_third(self):
+        self.q_ring.arrived()
 
     def p_first(self):
-        self.arrived()
-        self.ring_first(self.p_spot, self.place.along_p)
+        self.p_ring.first()
         self.share(0)
 
     def p_second(self):
-        self.arrived()
-        self.ring_second(self.p_spot, self.place.along_p)
+        self.p_ring.second()
         self.share(1)
         self.share(3)
 
     def p_third(self):
-        self.arrived()
+        self.p_ring.arrived()
         self.share(2)
 
     def finish(self):
         for copy in self.to_core:
             copy.wait_recv()
 
-    def ring_first(self, spot, along):
-        whole = pl.ds(0, SHARDS)
-        own = spot(0, whole)
-        self.stage = [
-            self.copies.start(own, own, along(1)),
-            self.copies.start(own, own, along(3)),
-        ]
-
-    def ring_second(self, spot, along):
-        low, high = pl.ds(0, SHARDS // 2), pl.ds(SHARDS // 2, SHARDS // 2)
-        self.stage = [
-            self.copies.start(spot(3, low), spot(3, low), along(1)),
-            self.copies.start(spot(1, high), spot(1, high), along(3)),
-        ]
-
     def share(self, step):
-        if self.both:
-            block = self.p_spot(step, pl.ds(0, SHARDS))
-            self.to_core.append(self.copies.start(block, block, self.place.sibling()))
+        block = self.p_spot(step, pl.ds(0, SHARDS))
+        self.to_core.append(self.copies.start(block, block, self.place.sibling()))
+
+
+def cols(q):
+    return pl.ds(pl.multiple_of(q * COLS, COLS), COLS)
+
+
+def renew_stat(place, grad, stat, out):
+    mine = cols(place.q)
+
+    def keep(pair, outer):
+        new = BETA_STAT * stat[pair] + (1.0 - BETA_STAT) * outer.reshape(2, ROWS, COLS)
+        out[pair, :, mine] = new.astype(jnp.bfloat16)
+
+    @pl.when(place.core == 0)
+    def _():
+        other = grad[pl.ds(2 * place.q, 2)].reshape(COLS, ORDER)
+
+        @pl.loop(0, SHARDS // 2)
+        def _(index):
+            pair = pl.ds(2 * index, 2)
+            keep(pair, contract_cols(grad[pair].reshape(COLS, ORDER), other))
+
+    @pl.when(place.core == 1)
+    def _():
+        other = grad[:, :, mine].reshape(ORDER, COLS)
+
+        @pl.loop(0, SHARDS // 2)
+        def _(index):
+            block = grad[:, :, cols(index)].reshape(ORDER, COLS)
+            keep(pl.ds(2 * index, 2), contract_rows(block, other))
 
 
 def collect_kernel(
     grads, moment, stat, base_left, base_right,
-    out_grad, out_moment, out_left, out_right, out_stat,
+    out_left, out_right, out_turned, out_stat,
+    all_grad, all_moment, all_stat,
     recv0, acc0, recv1, acc1, recv2, acc2, recv3, grad_piece, moment_piece,
     send, recv, local,
 ):
@@ -202,23 +244,33 @@
     half = ROWS // 2
     mine = pl.ds(pl.multiple_of(place.core * half, half), half)
     theirs = pl.ds(pl.multiple_of((1 - place.core) * half, half), half)
-    g, m, l, r, s = [
-        Gather(place, copies, local.at[index], out, both)
-        for index, (out, both) in enumerate(
-            (
-                (out_grad, True),
-                (out_moment, True),
-                (out_left, True),
-                (out_right, True),
-                (out_stat, False),
-            )
-        )
+    g, m, l, r, t = [
+        Gather(place, copies, local.at[index], out)
+        for index, out in enumerate((all_grad, all_moment, out_left, out_right, out_turned))
     ]
+
+    def quarter(p):
+        return pl.ds(pl.multiple_of(p * (ROWS // SIDE), ROWS // SIDE), ROWS // SIDE)
+
+    def stat_p_spot(step, zs):
+        return all_stat.at[zs, quarter(lax.rem(place.p + step, SIDE)), :]
+
+    def stat_q_spot(step, zs):
+        return out_stat.at[zs, :, cols(lax.rem(place.q + step, SIDE))]
+
+    s_in = Ring(copies, stat_p_spot, place.along_p)
+    s_out = Ring(copies, stat_q_spot, place.along_q)
 
     core_copy = copies.start(grads.at[theirs, :], recv0, place.sibling())
     l.z_stage(l.piece(base_left))
     r.z_stage(r.piece(base_right))
-    s.z_stage(s.piece(stat))
+    s_spread = Spread(
+        place,
+        copies,
+        stat.at[quarter(place.p), cols(place.q)],
+        all_stat.at[place.z, quarter(place.p), :],
+        local.at[5],
+    )
 
     core_copy.wait_recv()
     acc0[...] = (
@@ -235,7 +287,7 @@
     acc1[...] = (acc0[place.p] + recv1[0]) + (recv1[1] + recv1[2])
     q_copies = [
         copies.start(
-            acc1.at[:, g.cols(lax.rem(place.q + step, SIDE))],
+            acc1.at[:, cols(lax.rem(place.q + step, SIDE))],
             recv2.at[step - 1],
             place.along_q(step),
         )
@@ -243,14 +295,14 @@
     ]
     for copy in q_copies:
         copy.wait_recv()
-    acc2[...] = (acc1[:, g.cols(place.q)] + recv2[0]) + (recv2[1] + recv2[2])
+    acc2[...] = (acc1[:, cols(place.q)] + recv2[0]) + (recv2[1] + recv2[2])
     far_copy = copies.start(acc2, recv3, place.far())
     l.q_first()
     r.q_first()
     far_copy.wait_recv()
     piece = (acc2[...] + recv3[...]).astype(jnp.bfloat16)
     grad_piece[...] = piece
-    old = moment[g.rows(place.p), g.cols(place.q)]
+    old = moment[g.rows(place.p), cols(place.q)]
     moment_piece[...] = (
         BETA_ONE * old + (1.0 - BETA_ONE) * piece.astype(jnp.float32)
     ).astype(jnp.bfloat16)
@@ -259,45 +311,68 @@
 
     l.q_second()
     r.q_second()
-    s.q_first()
+    l.q_third()
     l.p_first()
+    r.q_third()
     r.p_first()
-    s.q_second()
+    s_spread.arrived()
+    s_in.first()
     g.q_first()
     m.q_first()
-    s.p_first()
+    r.p_second()
+    l.p_second()
+    s_in.second()
     g.q_second()
     m.q_second()
-    l.p_second()
-    r.p_second()
+    r.p_third()
+    l.p_third()
+    g.q_third()
     g.p_first()
-    m.p_first()
-    l.p_third()
-    r.p_third()
-    s.p_second()
+    m.q_third()
+    r.finish()
+    own = g.rows(place.p)
+    height = ROWS // SIDE // 2
+    pair = jnp.concatenate(
+        [all_grad[:, own, :].reshape(ROWS, ORDER), all_moment[:, own, :].reshape(ROWS, ORDER)]
+    )
+    right_cols = out_right[:, :, pl.ds(pl.multiple_of(place.z * ROWS, ROWS), ROWS)]
+    turned = jnp.dot(
+        pair, right_cols.reshape(ORDER, ROWS), preferred_element_type=jnp.float32
+    ).astype(jnp.bfloat16)
+    out_turned[:, own, :ROWS] = turned[:ROWS].reshape(SHARDS, height, ROWS)
+    out_turned[:, own, ROWS:] = turned[ROWS:].reshape(SHARDS, height, ROWS)
     g.p_second()
-    m.p_second()
+    t.p_first()
     g.p_third()
-    m.p_third()
-    s.p_third()
-    for gather in (l, r, g, m):
-        gather.finish()
+    t.p_second()
+    s_in.arrived()
+    g.finish()
+    renew_stat(place, all_grad, all_stat, out_stat)
+    s_out.first()
+    t.p_third()
+    s_out.second()
+    s_out.arrived()
+    l.finish()
+    t.finish()
     copies.finish()
 
 
 def collect(grads, moment, stat, base_left, base_right):
     whole = (SHARDS, ROWS, ORDER)
+    part = (SHARDS, ROWS, COLS)
     vmem = pl.BlockSpec(memory_space=pltpu.VMEM)
-    outs = [jax.ShapeDtypeStruct(whole, jnp.bfloat16)] * 4
-    outs += [jax.ShapeDtypeStruct(whole, jnp.float32)]
+    outs = [jax.ShapeDtypeStruct(shape, jnp.bfloat16) for shape in (whole, whole, part, whole)]
     height = ROWS // SIDE // 2
     f32, bf16 = jnp.float32, jnp.bfloat16
     return pl.pallas_call(
         collect_kernel,
         out_shape=outs,
         in_specs=[vmem] * 5,
-        out_specs=[vmem] * 5,
+        out_specs=[vmem] * 4,
         scratch_shapes=[
+            pltpu.VMEM(whole, bf16),
+            pltpu.VMEM(whole, bf16),
+            pltpu.VMEM(part, f32),
             pltpu.VMEM((ROWS // 2, ORDER), bf16),
             pltpu.VMEM((SIDE, height, ORDER), f32),
             pltpu.VMEM((SIDE - 1, height, ORDER), f32),
@@ -321,40 +396,25 @@
     core = lax.rem(lax.axis_index("dp"), 2)
     is_left = core == 0
     row_start = position * ROWS
-    gradient, moment_half, left_rot, right_rot, stat = collect(
+    left_rot, right_rot, turned, stat_new = collect(
         group_grads[0],
         moment,
         jnp.where(is_left, stat_left, stat_right),
         basis_left.astype(jnp.bfloat16),
         basis_right.astype(jnp.bfloat16),
     )
-    gradient, moment_half, left_rot, right_rot, stat = [
-        array.reshape(ORDER, ORDER)
-        for array in (gradient, moment_half, left_rot, right_rot, stat)
+    left_rot, right_rot, turned, stat_new = [
+        array.reshape(ORDER, -1) for array in (left_rot, right_rot, turned, stat_new)
     ]
 
-    right_cols = lax.dynamic_slice_in_dim(right_rot, row_start, ROWS, 1)
-    grad_block = jnp.dot(gradient, right_cols, preferred_element_type=jnp.float32).astype(
-        jnp.bfloat16
-    )
-    moment_block = jnp.dot(moment_half, right_cols, preferred_element_type=jnp.float32).astype(
-        jnp.bfloat16
-    )
-    grad_rot = contract_rows(left_rot, grad_block) / ORDER
-    moment_rot = contract_rows(left_rot, moment_block) / ORDER
+    rotated = contract_rows(left_rot, turned) / ORDER
+    grad_rot, moment_rot = rotated[:, :ROWS], rotated[:, ROWS:]
     second_new = BETA_TWO * second + (1.0 - BETA_TWO) * grad_rot * grad_rot
     scaled = (moment_rot / (jnp.sqrt(second_new) + EPSILON)).astype(jnp.bfloat16)
     turned_back = jnp.dot(left_rot, scaled, preferred_element_type=jnp.float32).astype(jnp.bfloat16)
     back_rows = lax.all_to_all(turned_back, "shard", split_axis=0, concat_axis=1, tiled=True)
     update = (contract_cols(back_rows, right_rot) / ORDER).astype(jnp.bfloat16)
 
-    outer = lax.cond(
-        is_left,
-        lambda g: contract_cols(g, g),
-        lambda g: contract_rows(g, g),
-        gradient,
-    )
-    stat_new = (BETA_STAT * stat + (1.0 - BETA_STAT) * outer).astype(jnp.bfloat16)
     rot = jnp.where(is_left, left_rot, right_rot)
     product = jnp.dot(stat_new, rot, preferred_element_type=jnp.float32)
     squares = jnp.sum(product * product, axis=0)

time: 154 us -> 139 us (0.903)
  matrix products: 33.5 us -> 24.5 us
  Pallas kernels: 96.7 us -> 88 us
  starting transfers between devices: 8.75 us -> 15.1 us
  other arithmetic: 10.6 us -> 6.84 us
    dot_general x3 -> x1, matrix products: 15.2 us -> 2.56 us  [contract_rows(): lax.dot_general(left_mat, right_mat, (((0,), (0,)), ((), ())), preferred_...]
    pallas_call x1, Pallas kernels: 96.7 us -> 88 us  [collect(): pl.pallas_call(collect_kernel, out_shape=outs, in_specs=[vmem] * 5, out_s...]
    all_to_all x1, starting transfers between devices: 6.46 us -> 11.5 us  [body(): lax.all_to_all(turned_back, 'shard', split_axis=0, concat_axis=1, tiled=T...]
    dot_general x2, matrix products: 11.8 us -> 15.4 us  [body(): jnp.dot(gram, current, preferred_element_type=jnp.float32)]
    mul x1 -> x0, other arithmetic: 2.83 us -> none  [body(): BETA_STAT * stat + (1.0 - BETA_STAT) * outer]
  transfers between devices with their start and end apart: 2 -> 2, of which waited for: 1 -> 1; matrix products, arithmetic and copies ran while one was open for 18% -> 15% of each run, Pallas kernels for 0% -> 0%
where the time goes in v2:
time: 139 us
  Pallas kernels  88 us (63%)
  matrix products  24.5 us (18%)
  starting transfers between devices  15.1 us (11%)
  other arithmetic  6.84 us (5%)
  local copies, waits for them, and re-layouts  2.22 us (2%)
  waiting for transfers between devices  1.52 us (1%)
    pallas_call x1, Pallas kernels, collect(): pl.pallas_call(collect_kernel, out_shape=outs, in_specs=[vmem] * 5, out_s...  88 us
    dot_general x2, matrix products, body(): jnp.dot(gram, current, preferred_element_type=jnp.float32)  15.4 us
    all_to_all x1, starting transfers between devices, body(): lax.all_to_all(turned_back, 'shard', split_axis=0, concat_axis=1, tiled=T...  11.5 us
    dot_general x1, matrix products, body(): product = jnp.dot(stat_new, rot, preferred_element_type=jnp.float32)  4.27 us
    ppermute x1, starting transfers between devices, body(): other = lax.ppermute(result, 'dp', [(i, i ^ 1) for i in range(size)])  3.55 us
  transfers between devices with their start and end apart: 2, of which 1 were waited for; matrix products, arithmetic and copies ran while one was open for 15% of the time, Pallas kernels for 0%

profile of v2, /device:TPU:1, one launch (start us, length us, event | category | flops | bytes accessed | tf_op | source)
XLA Modules:
  0.0 138.9 jit_solution(11459712896942116553)
XLA Ops:
  0.6 1.8 %convert_element_type.33.base_left = bf16[128,1024]{1,0:T(8,128)(2,1)} convert(f32[128,1024]{1,0:T(8,128)} %param.12) | non-fusion elementwise | flops 131072 | bytes 786432 | tf_op jit(solution)/shard_map/convert_element_type | solution.py:403
  2.4 1.8 %convert_element_type.34.base_right = bf16[128,1024]{1,0:T(8,128)(2,1)} convert(f32[128,1024]{1,0:T(8,128)} %param.13) | non-fusion elementwise | flops 131072 | bytes 786432 | tf_op jit(solution)/shard_map/convert_element_type | solution.py:404
  4.2 1.9 %broadcast_select_fusion.3.stat = f32[128,1024]{1,0:T(8,128)} fusion(f32[128,1024]{1,0:T(8,128)} %param.10, f32[128,1024]{1,0:T(8,128)} %param.11, pred[]{:T(512)S(6)} %eq.3), kind=kLoop, calls=%fused_computation.23 | loop fusion | flops 131072 | bytes 1572865 | tf_op jit(solution)/shard_map/jit(_where)/select_n | solution.py:402
  6.1 88.0 %collect.1 = (bf16[8,128,1024]{2,1,0:T(8,128)(2,1)}, bf16[8,128,1024]{2,1,0:T(8,128)(2,1)}, bf16[8,128,256]{2,1,0:T(8,128)(2,1)}, bf16[8,128,1024]{2,1,0:T(8,128)(2,1)}) custom-call(bf16[128,1024]{1,0:T(8,128)(2,1)} %bitcast.26, f32[128,1024]{1,0:T(8,128)} %moment.1, f32[128,1024]{1,0:T(8,128)} %broadcast_select_fusion.3.stat, ...), custom_call_target="tpu_custom_call" | custom-call | tf_op jit(solution)/shard_map/collect/pallas_call | solution.py:367
  94.1 0.0 copy-start.2
  94.1 0.0 copy-start.1
  94.1 2.6 %fusion = f32[1024,256]{1,0:T(8,128)S(1)} fusion(bf16[8,128,1024]{2,1,0:T(8,128)(2,1)} %get-tuple-element.8, bf16[8,128,256]{2,1,0:T(8,128)(2,1)} %get-tuple-element.9), kind=kOutput, calls=%fused_computation.6 | convolution fusion | flops 537133056 | bytes 3670016 | tf_op jit(solution)/shard_map/dot_general | solution.py:27
  96.7 0.0 copy-done.2
  96.7 0.1 fusion.4
  96.8 0.0 copy-start.3
  96.8 0.0 copy-done.1
  96.8 0.0 copy-start
  96.8 0.8 convolution_convert_fusion
  97.6 0.0 copy-done.3
  97.6 0.9 copy.13
  98.5 11.5 %all-to-all-start = ((bf16[8,128,128]{1,2,0:T(8,128)(2,1)}), bf16[8,128,128]{1,2,0:T(8,128)(2,1)S(1)}, u32[]{:S(2)}, u32[]{:S(2)}) async-start(bf16[8,128,128]{1,2,0:T(8,128)(2,1)} %copy.13), calls=%async_computation | async-start | bytes 524288 | tf_op jit(solution)/shard_map/all_to_all | solution.py:415
  110.0 0.0 copy-done
  110.0 0.0 copy-start.4
  110.0 0.2 broadcast_select_fusion
  110.3 1.3 copy-done.4
  111.6 4.3 %multiply_reduce_fusion = (f32[1024]{0:T(1024)S(1)}, f32[1024,1024]{1,0:T(8,128)}) fusion(bf16[1024,1024]{1,0:T(8,128)(2,1)S(1)} %bitcast.28, bf16[1024,1024]{1,0:T(8,128)(2,1)S(1)} %bitcast.24), kind=kOutput, calls=%fused_computation.3 | convolution fusion | flops 2149579776 | bytes 8392704 | tf_op jit(solution)/shard_map/dot_general | solution.py:419
  115.9 12.0 %subtract_convert_fusion = bf16[1024,1024]{1,0:T(8,128)(2,1)} fusion(f32[1024,1024]{1,0:T(8,128)} %get-tuple-element.15, f32[1024]{0:T(1024)S(1)} %add_sqrt_fusion), kind=kOutput, calls=%fused_computation | convolution fusion | flops 4308598784 | bytes 6295552 | tf_op jit(solution)/shard_map/dot_general | solution.py:426
  127.8 3.4 %fusion.1 = f32[128,1024]{1,0:T(8,128)S(1)} fusion(bf16[1024,1024]{1,0:T(8,128)(2,1)} %subtract_convert_fusion, s32[]{:T(128)S(6)} %select_n.35), kind=kOutput, calls=%fused_computation.8 | convolution fusion | flops 537657344 | bytes 5243904 | tf_op jit(solution)/shard_map/dot_general | solution.py:430
  131.3 3.6 %collective-permute-start = (f32[128,1024]{1,0:T(8,128)S(1)}, f32[128,1024]{1,0:T(8,128)S(1)}, u32[]{:S(2)}, u32[]{:S(2)}) collective-permute-start(f32[128,1024]{1,0:T(8,128)S(1)} %fusion.1), channel_id=1, source_target_pairs={{0,8},{8,0},{16,24},{24,16},{32,40},{40,32},{48,56},{56,48},{64,72... | collective-permute-start | bytes 1572872 | tf_op jit(solution)/shard_map/ppermute | solution.py:434
  134.8 1.5 %collective-permute-done = f32[128,1024]{1,0:T(8,128)S(1)} collective-permute-done((f32[128,1024]{1,0:T(8,128)S(1)}, f32[128,1024]{1,0:T(8,128)S(1)}, u32[]{:S(2)}, u32[]{:S(2)}) %collective-permute-start) | collective-permute-done | bytes 524320 | tf_op jit(solution)/shard_map/ppermute | solution.py:434
  136.3 1.1 broadcast_select_fusion.1
  137.4 0.0 all-to-all-done
  137.4 1.5 %fusion.2 = bf16[128,1024]{1,0:T(8,128)(2,1)} fusion(bf16[128,1024]{0,1:T(8,128)(2,1)S(1)} %bitcast.25, bf16[1024,1024]{1,0:T(8,128)(2,1)S(1)} %bitcast.22), kind=kOutput, calls=%fused_computation.12 | convolution fusion | flops 268697600 | bytes 2621440 | tf_op jit(solution)/shard_map/dot_general | solution.py:33
  (1 shorter events, 0.0 us)
Async XLA Ops:
  94.1 2.6 %copy-start.2 = (f32[1024,128]{1,0:T(8,128)S(1)}, f32[1024,128]{1,0:T(8,128)}, u32[]{:S(2)}) copy-start(f32[1024,128]{1,0:T(8,128)} %param.9) | copy-start | bytes 1572868
  94.1 2.7 %copy-start.1 = (bf16[8,128,1024]{2,1,0:T(8,128)(2,1)S(1)}, bf16[8,128,1024]{2,1,0:T(8,128)(2,1)}, u32[]{:S(2)}) copy-start(bf16[8,128,1024]{2,1,0:T(8,128)(2,1)} %get-tuple-element.8) | copy-start | bytes 6291460
  96.8 0.8 copy-start.3
  96.8 13.2 %copy-start = (bf16[8,128,1024]{2,1,0:T(8,128)(2,1)S(1)}, bf16[8,128,1024]{2,1,0:T(8,128)(2,1)}, u32[]{:S(2)}) copy-start(bf16[8,128,1024]{2,1,0:T(8,128)(2,1)} %get-tuple-element.10) | copy-start | bytes 6291460
  98.5 38.9 %all-to-all-start = ((bf16[8,128,128]{1,2,0:T(8,128)(2,1)}), bf16[8,128,128]{1,2,0:T(8,128)(2,1)S(1)}, u32[]{:S(2)}, u32[]{:S(2)}) async-start(bf16[8,128,128]{1,2,0:T(8,128)(2,1)} %copy.13), calls=%async_computation | async-start | bytes 524288 | tf_op jit(solution)/shard_map/all_to_all | solution.py:415
  110.0 1.6 %copy-start.4 = (bf16[8,128,1024]{2,1,0:T(8,128)(2,1)S(1)}, bf16[8,128,1024]{2,1,0:T(8,128)(2,1)}, u32[]{:S(2)}) copy-start(bf16[8,128,1024]{2,1,0:T(8,128)(2,1)} %get-tuple-element.11) | copy-start | bytes 6291460
  131.3 5.1 %collective-permute-start = (f32[128,1024]{1,0:T(8,128)S(1)}, f32[128,1024]{1,0:T(8,128)S(1)}, u32[]{:S(2)}, u32[]{:S(2)}) collective-permute-start(f32[128,1024]{1,0:T(8,128)S(1)} %fusion.1), channel_id=1, source_target_pairs={{0,8},{8,0},{16,24},{24,16},{32,40},{40,32},{48,56},{56,48},{64,72... | collective-permute-start | bytes 1572872 | tf_op jit(solution)/shard_map/ppermute | solution.py:434

commit v3 on v2

--- a/solution.py
+++ b/solution.py
@@ -19,8 +19,8 @@
 ROWS = ORDER // SHARDS
 SIDE = 4
 COLS = ORDER // SIDE
-COPIES = 100
-LOCALS = 6
+COPIES = 120
+LOCALS = 13
 
 
 def contract_rows(left_mat, right_mat):
@@ -195,6 +195,65 @@
     return pl.ds(pl.multiple_of(q * COLS, COLS), COLS)
 
 
+def columns_of(ref, index):
+    return ref[:, :, cols(index)].reshape(ORDER, COLS)
+
+
+def rows_of(ref, index):
+    return ref[pl.ds(2 * index, 2)].reshape(COLS, ORDER)
+
+
+def full(ref):
+    return ref[...].reshape(ORDER, ORDER)
+
+
+def multiply(left_mat, right_mat):
+    return jnp.dot(left_mat, right_mat, preferred_element_type=jnp.float32)
+
+
+def rotate(left_rot, turned, second, out_second, scaled):
+    @pl.loop(0, SIDE)
+    def _(index):
+        rotated = contract_rows(columns_of(left_rot, index), turned[...].reshape(ORDER, COLS))
+        rotated = rotated / ORDER
+        grad_rot, moment_rot = rotated[:, :ROWS], rotated[:, ROWS:]
+        new = BETA_TWO * second[cols(index), :] + (1.0 - BETA_TWO) * grad_rot * grad_rot
+        out_second[cols(index), :] = new
+        scaled[cols(index), :] = (moment_rot / (jnp.sqrt(new) + EPSILON)).astype(jnp.bfloat16)
+
+
+def turn_back(left_rot, scaled, back):
+    @pl.loop(0, SIDE)
+    def _(index):
+        back[pl.ds(2 * index, 2)] = (
+            multiply(rows_of(left_rot, index), scaled[...])
+            .astype(jnp.bfloat16)
+            .reshape(2, ROWS, ROWS)
+        )
+
+
+def power_step(stat, rot, current):
+    @pl.loop(0, SIDE)
+    def _(index):
+        product = multiply(full(stat), columns_of(rot, index))
+        squares = jnp.sum(product * product, axis=0, keepdims=True)
+        start = product / jnp.sqrt(squares / ORDER + NORM_EPS)
+        current[:, :, cols(index)] = start.astype(jnp.bfloat16).reshape(SHARDS, ROWS, COLS)
+
+
+def newton_schulz(current, gram, later):
+    @pl.loop(0, SIDE)
+    def _(index):
+        block = contract_cols(full(current), rows_of(current, index)) / ORDER
+        gram[:, :, cols(index)] = block.astype(jnp.bfloat16).reshape(SHARDS, ROWS, COLS)
+
+    @pl.loop(0, SIDE)
+    def _(index):
+        mine = columns_of(current, index)
+        block = 1.5 * mine.astype(jnp.float32) - 0.5 * multiply(full(gram), mine)
+        later[:, :, cols(index)] = block.astype(jnp.bfloat16).reshape(SHARDS, ROWS, COLS)
+
+
 def renew_stat(place, grad, stat, out):
     mine = cols(place.q)
 
@@ -221,14 +280,53 @@
             keep(pl.ds(2 * index, 2), contract_rows(block, other))
 
 
-def collect_kernel(
-    grads, moment, stat, base_left, base_right,
-    out_left, out_right, out_turned, out_stat,
-    all_grad, all_moment, all_stat,
+def step_kernel(
+    grads, moment, second, stat_left, stat_right, base_left, base_right,
+    out_update, out_second, out_bases,
+    bases, all_grad, all_moment, all_turned, all_stat, new_stat,
+    current, gram, later, gram_rows, scaled, back, back_rows,
     recv0, acc0, recv1, acc1, recv2, acc2, recv3, grad_piece, moment_piece,
+    own_grads, own_second, old_moment, stat_pieces, base_pieces, sent_bases, stat_piece,
     send, recv, local,
 ):
     place = Place()
+    half = ROWS // 2
+    mine = pl.ds(pl.multiple_of(place.core * half, half), half)
+    theirs = pl.ds(pl.multiple_of((1 - place.core) * half, half), half)
+
+    def quarter(p):
+        return pl.ds(pl.multiple_of(p * (ROWS // SIDE), ROWS // SIDE), ROWS // SIDE)
+
+    copies = Copies(send, recv)
+    g, m, l, r, t = [
+        Gather(place, copies, local.at[index], out)
+        for index, out in enumerate(
+            (all_grad, all_moment, bases.at[0], bases.at[1], all_turned)
+        )
+    ]
+    stat_spot = (quarter(place.p), cols(place.q))
+    loads = [
+        pltpu.make_async_copy(src, dst, local.at[6 + index])
+        for index, (src, dst) in enumerate(
+            (
+                (l.piece(base_left), base_pieces.at[0]),
+                (r.piece(base_right), base_pieces.at[1]),
+                (stat_left.at[stat_spot], stat_pieces.at[0]),
+                (stat_right.at[stat_spot], stat_pieces.at[1]),
+                (grads.at[mine, :], own_grads),
+                (g.piece(moment), old_moment),
+                (second, own_second),
+            )
+        )
+    ]
+    for load in loads:
+        load.start()
+
+    for load in loads[:4]:
+        load.wait()
+    sent_bases[...] = base_pieces[...].astype(jnp.bfloat16)
+    stat_piece[...] = stat_pieces[place.core]
+
     barrier = pltpu.get_barrier_semaphore()
     partners = [place.sibling(), place.far()]
     partners += [place.along_p(step) for step in (1, 2, 3)]
@@ -240,41 +338,30 @@
         )
     pl.semaphore_wait(barrier, len(partners))
 
-    copies = Copies(send, recv)
-    half = ROWS // 2
-    mine = pl.ds(pl.multiple_of(place.core * half, half), half)
-    theirs = pl.ds(pl.multiple_of((1 - place.core) * half, half), half)
-    g, m, l, r, t = [
-        Gather(place, copies, local.at[index], out)
-        for index, out in enumerate((all_grad, all_moment, out_left, out_right, out_turned))
-    ]
-
-    def quarter(p):
-        return pl.ds(pl.multiple_of(p * (ROWS // SIDE), ROWS // SIDE), ROWS // SIDE)
-
     def stat_p_spot(step, zs):
         return all_stat.at[zs, quarter(lax.rem(place.p + step, SIDE)), :]
 
     def stat_q_spot(step, zs):
-        return out_stat.at[zs, :, cols(lax.rem(place.q + step, SIDE))]
+        return new_stat.at[zs, :, cols(lax.rem(place.q + step, SIDE))]
 
     s_in = Ring(copies, stat_p_spot, place.along_p)
     s_out = Ring(copies, stat_q_spot, place.along_q)
 
     core_copy = copies.start(grads.at[theirs, :], recv0, place.sibling())
-    l.z_stage(l.piece(base_left))
-    r.z_stage(r.piece(base_right))
+    l.z_stage(sent_bases.at[0])
+    r.z_stage(sent_bases.at[1])
     s_spread = Spread(
         place,
         copies,
-        stat.at[quarter(place.p), cols(place.q)],
+        stat_piece,
         all_stat.at[place.z, quarter(place.p), :],
         local.at[5],
     )
 
+    loads[4].wait()
     core_copy.wait_recv()
     acc0[...] = (
-        grads[mine, :].astype(jnp.float32) + recv0[...].astype(jnp.float32)
+        own_grads[...].astype(jnp.float32) + recv0[...].astype(jnp.float32)
     ).reshape(acc0.shape)
     p_copies = [
         copies.start(
@@ -302,7 +389,8 @@
     far_copy.wait_recv()
     piece = (acc2[...] + recv3[...]).astype(jnp.bfloat16)
     grad_piece[...] = piece
-    old = moment[g.rows(place.p), cols(place.q)]
+    loads[5].wait()
+    old = old_moment[...]
     moment_piece[...] = (
         BETA_ONE * old + (1.0 - BETA_ONE) * piece.astype(jnp.float32)
     ).astype(jnp.bfloat16)
@@ -335,44 +423,102 @@
     pair = jnp.concatenate(
         [all_grad[:, own, :].reshape(ROWS, ORDER), all_moment[:, own, :].reshape(ROWS, ORDER)]
     )
-    right_cols = out_right[:, :, pl.ds(pl.multiple_of(place.z * ROWS, ROWS), ROWS)]
+    right_cols = bases[1, :, :, pl.ds(pl.multiple_of(place.z * ROWS, ROWS), ROWS)]
     turned = jnp.dot(
         pair, right_cols.reshape(ORDER, ROWS), preferred_element_type=jnp.float32
     ).astype(jnp.bfloat16)
-    out_turned[:, own, :ROWS] = turned[:ROWS].reshape(SHARDS, height, ROWS)
-    out_turned[:, own, ROWS:] = turned[ROWS:].reshape(SHARDS, height, ROWS)
+    all_turned[:, own, :ROWS] = turned[:ROWS].reshape(SHARDS, height, ROWS)
+    all_turned[:, own, ROWS:] = turned[ROWS:].reshape(SHARDS, height, ROWS)
     g.p_second()
     t.p_first()
     g.p_third()
     t.p_second()
     s_in.arrived()
     g.finish()
-    renew_stat(place, all_grad, all_stat, out_stat)
+    renew_stat(place, all_grad, all_stat, new_stat)
     s_out.first()
     t.p_third()
-    s_out.second()
-    s_out.arrived()
     l.finish()
     t.finish()
+    loads[6].wait()
+    left_rot, right_rot = bases.at[0], bases.at[1]
+    rotate(left_rot, all_turned, own_second, out_second, scaled)
+    s_out.second()
+    turn_back(left_rot, scaled, back)
+    here = pl.ds(pl.multiple_of(place.z * ROWS, ROWS), ROWS)
+    back_copies = [
+        copies.start(
+            back.at[lax.rem(place.z + step, SHARDS)],
+            back_rows.at[:, here],
+            place.along_z(step),
+        )
+        for step in (7, 1, 6, 2, 5, 3, 4)
+    ]
+    back_rows[:, here] = back[place.z]
+    s_out.arrived()
+
+    rot = bases.at[place.core]
+    power_step(new_stat, rot, current)
+    for _ in range(NS_ITERS - 1):
+        newton_schulz(current, gram, later)
+        current, later = later, current
+    rows = current[place.z]
+
+    @pl.loop(0, SIDE)
+    def _(index):
+        block = contract_cols(rows, rows_of(current, index)) / ORDER
+        gram_rows[:, cols(index)] = block.astype(jnp.bfloat16)
+
+    result_copies = []
+    for index in range(SIDE):
+        span = slice(index * COLS, (index + 1) * COLS)
+        out_bases[place.core, :, span] = 1.5 * rows[:, span].astype(jnp.float32) - 0.5 * multiply(
+            gram_rows[...], current[:, :, span].reshape(ORDER, COLS)
+        )
+        block = out_bases.at[place.core, :, span]
+        result_copies.append(copies.start(block, block, place.sibling()))
+
+    for copy in back_copies:
+        copy.wait_recv()
+
+    @pl.loop(0, SIDE)
+    def _(index):
+        block = contract_cols(back_rows[...], rows_of(right_rot, index)) / ORDER
+        out_update[:, cols(index)] = block.astype(jnp.bfloat16)
+
+    for copy in result_copies:
+        copy.wait_recv()
     copies.finish()
 
 
-def collect(grads, moment, stat, base_left, base_right):
+def step(*operands):
     whole = (SHARDS, ROWS, ORDER)
     part = (SHARDS, ROWS, COLS)
-    vmem = pl.BlockSpec(memory_space=pltpu.VMEM)
-    outs = [jax.ShapeDtypeStruct(shape, jnp.bfloat16) for shape in (whole, whole, part, whole)]
     height = ROWS // SIDE // 2
     f32, bf16 = jnp.float32, jnp.bfloat16
     return pl.pallas_call(
-        collect_kernel,
-        out_shape=outs,
-        in_specs=[vmem] * 5,
-        out_specs=[vmem] * 4,
+        step_kernel,
+        out_shape=[
+            jax.ShapeDtypeStruct((ROWS, ORDER), bf16),
+            jax.ShapeDtypeStruct((ORDER, ROWS), f32),
+            jax.ShapeDtypeStruct((2, ROWS, ORDER), f32),
+        ],
+        in_specs=[pl.BlockSpec(memory_space=pl.ANY)] * 7,
+        out_specs=[pl.BlockSpec(memory_space=pltpu.VMEM)] * 3,
         scratch_shapes=[
+            pltpu.VMEM((2, *whole), bf16),
             pltpu.VMEM(whole, bf16),
             pltpu.VMEM(whole, bf16),
+            pltpu.VMEM(part, bf16),
             pltpu.VMEM(part, f32),
+            pltpu.VMEM(whole, bf16),
+            pltpu.VMEM(whole, bf16),
+            pltpu.VMEM(whole, bf16),
+            pltpu.VMEM(whole, bf16),
+            pltpu.VMEM((ROWS, ORDER), bf16),
+            pltpu.VMEM((ORDER, ROWS), bf16),
+            pltpu.VMEM((SHARDS, ROWS, ROWS), bf16),
+            pltpu.VMEM((ROWS, ORDER), bf16),
             pltpu.VMEM((ROWS // 2, ORDER), bf16),
             pltpu.VMEM((SIDE, height, ORDER), f32),
             pltpu.VMEM((SIDE - 1, height, ORDER), f32),
@@ -382,59 +528,27 @@
             pltpu.VMEM((height, COLS), f32),
             pltpu.VMEM((height, COLS), bf16),
             pltpu.VMEM((height, COLS), bf16),
+            pltpu.VMEM((ROWS // 2, ORDER), bf16),
+            pltpu.VMEM((ORDER, ROWS), f32),
+            pltpu.VMEM((height, COLS), f32),
+            pltpu.VMEM((2, 2 * height, COLS), f32),
+            pltpu.VMEM((2, height, COLS), f32),
+            pltpu.VMEM((2, height, COLS), bf16),
+            pltpu.VMEM((2 * height, COLS), f32),
             pltpu.SemaphoreType.DMA((COPIES,)),
             pltpu.SemaphoreType.DMA((COPIES,)),
             pltpu.SemaphoreType.DMA((LOCALS,)),
         ],
         compiler_params=pltpu.CompilerParams(collective_id=0, has_side_effects=True),
-        name="collect",
-    )(grads, moment, stat, base_left, base_right)
+        name="step",
+    )(*operands)
 
 
 def body(group_grads, moment, second, stat_left, stat_right, basis_left, basis_right):
-    position = lax.axis_index("shard")
-    core = lax.rem(lax.axis_index("dp"), 2)
-    is_left = core == 0
-    row_start = position * ROWS
-    left_rot, right_rot, turned, stat_new = collect(
-        group_grads[0],
-        moment,
-        jnp.where(is_left, stat_left, stat_right),
-        basis_left.astype(jnp.bfloat16),
-        basis_right.astype(jnp.bfloat16),
+    update, second_new, bases = step(
+        group_grads[0], moment, second, stat_left, stat_right, basis_left, basis_right
     )
-    left_rot, right_rot, turned, stat_new = [
-        array.reshape(ORDER, -1) for array in (left_rot, right_rot, turned, stat_new)
-    ]
-
-    rotated = contract_rows(left_rot, turned) / ORDER
-    grad_rot, moment_rot = rotated[:, :ROWS], rotated[:, ROWS:]
-    second_new = BETA_TWO * second + (1.0 - BETA_TWO) * grad_rot * grad_rot
-    scaled = (moment_rot / (jnp.sqrt(second_new) + EPSILON)).astype(jnp.bfloat16)
-    turned_back = jnp.dot(left_rot, scaled, preferred_element_type=jnp.float32).astype(jnp.bfloat16)
-    back_rows = lax.all_to_all(turned_back, "shard", split_axis=0, concat_axis=1, tiled=True)
-    update = (contract_cols(back_rows, right_rot) / ORDER).astype(jnp.bfloat16)
-
-    rot = jnp.where(is_left, left_rot, right_rot)
-    product = jnp.dot(stat_new, rot, preferred_element_type=jnp.float32)
-    squares = jnp.sum(product * product, axis=0)
-    current = (product / jnp.sqrt(squares / ORDER + NORM_EPS)).astype(jnp.bfloat16)
-    for _ in range(NS_ITERS - 1):
-        gram = (contract_cols(current, current) / ORDER).astype(jnp.bfloat16)
-        current = (
-            1.5 * current.astype(jnp.float32)
-            - 0.5 * jnp.dot(gram, current, preferred_element_type=jnp.float32)
-        ).astype(jnp.bfloat16)
-    rows = lax.dynamic_slice_in_dim(current, row_start, ROWS, 0)
-    gram = (contract_cols(rows, current) / ORDER).astype(jnp.bfloat16)
-    result = 1.5 * rows.astype(jnp.float32) - 0.5 * jnp.dot(
-        gram, current, preferred_element_type=jnp.float32
-    )
-    size = lax.axis_size("dp")
-    other = lax.ppermute(result, "dp", [(i, i ^ 1) for i in range(size)])
-    left_result = jnp.where(is_left, result, other)
-    right_result = jnp.where(is_left, other, result)
-    return (update, second_new, left_result, right_result)
+    return (update, second_new, bases[0], bases[1])
 
 
 def solution(mesh):

time: 139 us -> 106 us (0.76)
  matrix products: 24.5 us -> 0 us
  starting transfers between devices: 15.1 us -> 0 us
  Pallas kernels: 88 us -> 99.8 us
  other arithmetic: 6.84 us -> 0 us
  local copies, waits for them, and re-layouts: 2.22 us -> 4.25 us
  waiting for transfers between devices: 1.52 us -> 0 us
    dot_general x6 -> x0, matrix products: 24.5 us -> none  [the longest x2 15.4 us: body(): jnp.dot(gram, current, preferred_element_type=jnp.float32)]
    pallas_call x1, Pallas kernels: 88 us -> 99.8 us  [step(): pl.pallas_call(step_kernel, out_shape=[jax.ShapeDtypeStruct((ROWS, ORDER)...]
    all_to_all x1 -> x0, starting transfers between devices: 11.5 us -> none  [body(): lax.all_to_all(turned_back, 'shard', split_axis=0, concat_axis=1, tiled=T...]
    convert_element_type x2 -> x0, other arithmetic: 3.56 us -> none  [the longest x1 1.78 us: body(): basis_left.astype(jnp.bfloat16)]
    ppermute x1 -> x0, starting transfers between devices: 3.55 us -> none  [body(): other = lax.ppermute(result, 'dp', [(i, i ^ 1) for i in range(size)])]
    select_n x3 -> x0, other arithmetic: 3.19 us -> none  [the longest x1 1.9 us: body(): jnp.where(is_left, stat_left, stat_right)]
    squeeze x0 -> x1, local copies, waits for them, and re-layouts: none -> 2.32 us  [body(): return (update, second_new, bases[0], bases[1])]
    ppermute x1 -> x0, waiting for transfers between devices: 1.51 us -> none  [body(): other = lax.ppermute(result, 'dp', [(i, i ^ 1) for i in range(size)])]
  transfers between devices with their start and end apart: 2 -> 0, of which waited for: 1 -> 0; matrix products, arithmetic and copies ran while one was open for 15% -> 0% of each run, Pallas kernels for 0% -> 0%
where the time goes in v3:
time: 106 us; the launch traced here: 105 us
  Pallas kernels  99.8 us (94%)
  local copies, waits for them, and re-layouts  4.25 us (4%)
    pallas_call x1, Pallas kernels, step(): pl.pallas_call(step_kernel, out_shape=[jax.ShapeDtypeStruct((ROWS, ORDER)...  99.8 us
    squeeze x1, local copies, waits for them, and re-layouts, body(): return (update, second_new, bases[0], bases[1])  2.32 us

profile of v3, /device:TPU:1, one launch (start us, length us, event | category | flops | bytes accessed | tf_op | source)
XLA Modules:
  0.0 104.7 jit_solution(6420237375995270428)
XLA Ops:
  0.6 99.8 %step.1 = (bf16[128,1024]{1,0:T(8,128)(2,1)}, f32[1024,128]{1,0:T(8,128)}, f32[2,128,1024]{2,1,0:T(8,128)}) custom-call(bf16[128,1024]{1,0:T(8,128)(2,1)} %bitcast.5, f32[128,1024]{1,0:T(8,128)} %moment.1, f32[1024,128]{1,0:T(8,128)} %second.1, f32[128,1024]{1,0:T(8,128)} %stat_left.1, f32[128,1024]{1,0:T(8,128)} %stat_right.1, f32[128,1024]{1,0:T(8,128)} %base_left.1, ...), custom_call_target="tpu_custom_call" | custom-call | tf_op jit(solution)/shard_map/step/pallas_call | solution.py:499
  100.5 0.0 copy-start.1
  100.5 2.3 %slice_bitcast_fusion = (f32[128,1024]{1,0:T(8,128)}, f32[128,1024]{1,0:T(8,128)}) fusion(f32[2,128,1024]{2,1,0:T(8,128)} %get-tuple-element.9), kind=kLoop, calls=%fused_computation | loop fusion | bytes 2097152 | tf_op jit(solution)/shard_map/squeeze | solution.py:551
  102.8 0.0 copy-start
  102.8 0.0 copy-done.1
  102.8 0.7 copy.13
  103.5 0.4 copy-done
  103.9 0.8 copy.14
Async XLA Ops:
  100.5 2.3 %copy-start.1 = (bf16[128,1024]{1,0:T(8,128)(2,1)S(1)}, bf16[128,1024]{1,0:T(8,128)(2,1)}, u32[]{:S(2)}) copy-start(bf16[128,1024]{1,0:T(8,128)(2,1)} %get-tuple-element.16) | copy-start | bytes 786436
  102.8 1.1 %copy-start = (f32[1024,128]{1,0:T(8,128)S(1)}, f32[1024,128]{1,0:T(8,128)}, u32[]{:S(2)}) copy-start(f32[1024,128]{1,0:T(8,128)} %get-tuple-element.17) | copy-start | bytes 1572868

commit v4 on v3

--- a/solution.py
+++ b/solution.py
@@ -63,6 +63,14 @@
         z = lax.rem(self.z + step, SHARDS)
         return (self.at(self.p, self.q, self.zhi, self.core), z)
 
+    def across_p(self, step):
+        p = lax.rem(self.p + step, SIDE)
+        return (self.at(p, self.q, self.zhi, 1 - self.core), self.z)
+
+    def across_q(self, step):
+        q = lax.rem(self.q + step, SIDE)
+        return (self.at(self.p, q, self.zhi, 1 - self.core), self.z)
+
     def far(self):
         return (self.at(self.p, self.q, 1 - self.zhi, self.core), self.z)
 
@@ -192,6 +200,8 @@
 
 
 def cols(q):
+    if isinstance(q, int):
+        return pl.ds(q * COLS, COLS)
     return pl.ds(pl.multiple_of(q * COLS, COLS), COLS)
 
 
@@ -212,8 +222,7 @@
 
 
 def rotate(left_rot, turned, second, out_second, scaled):
-    @pl.loop(0, SIDE)
-    def _(index):
+    for index in range(SIDE):
         rotated = contract_rows(columns_of(left_rot, index), turned[...].reshape(ORDER, COLS))
         rotated = rotated / ORDER
         grad_rot, moment_rot = rotated[:, :ROWS], rotated[:, ROWS:]
@@ -223,8 +232,7 @@
 
 
 def turn_back(left_rot, scaled, back):
-    @pl.loop(0, SIDE)
-    def _(index):
+    for index in range(SIDE):
         back[pl.ds(2 * index, 2)] = (
             multiply(rows_of(left_rot, index), scaled[...])
             .astype(jnp.bfloat16)
@@ -232,23 +240,29 @@
         )
 
 
-def power_step(stat, rot, current):
-    @pl.loop(0, SIDE)
-    def _(index):
-        product = multiply(full(stat), columns_of(rot, index))
-        squares = jnp.sum(product * product, axis=0, keepdims=True)
-        start = product / jnp.sqrt(squares / ORDER + NORM_EPS)
-        current[:, :, cols(index)] = start.astype(jnp.bfloat16).reshape(SHARDS, ROWS, COLS)
+def quarter_product(place, stat, rot, steps, index):
+    total = None
+    for step in steps:
+        part = lax.rem(place.q + step, SIDE)
+        term = multiply(
+            columns_of(stat, part), rot[pl.ds(2 * part, 2), :, cols(index)].reshape(COLS, COLS)
+        )
+        total = term if total is None else total + term
+    return total
+
+
+def normalize(product):
+    squares = jnp.sum(product * product, axis=0, keepdims=True)
+    start = product / jnp.sqrt(squares / ORDER + NORM_EPS)
+    return start.astype(jnp.bfloat16).reshape(SHARDS, ROWS, COLS)
 
 
 def newton_schulz(current, gram, later):
-    @pl.loop(0, SIDE)
-    def _(index):
+    for index in range(SIDE):
         block = contract_cols(full(current), rows_of(current, index)) / ORDER
         gram[:, :, cols(index)] = block.astype(jnp.bfloat16).reshape(SHARDS, ROWS, COLS)
 
-    @pl.loop(0, SIDE)
-    def _(index):
+    for index in range(SIDE):
         mine = columns_of(current, index)
         block = 1.5 * mine.astype(jnp.float32) - 0.5 * multiply(full(gram), mine)
         later[:, :, cols(index)] = block.astype(jnp.bfloat16).reshape(SHARDS, ROWS, COLS)
@@ -265,8 +279,7 @@
     def _():
         other = grad[pl.ds(2 * place.q, 2)].reshape(COLS, ORDER)
 
-        @pl.loop(0, SHARDS // 2)
-        def _(index):
+        for index in range(SIDE):
             pair = pl.ds(2 * index, 2)
             keep(pair, contract_cols(grad[pair].reshape(COLS, ORDER), other))
 
@@ -274,8 +287,7 @@
     def _():
         other = grad[:, :, mine].reshape(ORDER, COLS)
 
-        @pl.loop(0, SHARDS // 2)
-        def _(index):
+        for index in range(SIDE):
             block = grad[:, :, cols(index)].reshape(ORDER, COLS)
             keep(pl.ds(2 * index, 2), contract_rows(block, other))
 
@@ -285,14 +297,12 @@
     out_update, out_second, out_bases,
     bases, all_grad, all_moment, all_turned, all_stat, new_stat,
     current, gram, later, gram_rows, scaled, back, back_rows,
-    recv0, acc0, recv1, acc1, recv2, acc2, recv3, grad_piece, moment_piece,
+    product, recv1, acc1, recv2, acc2, recv3, grad_piece, moment_piece,
     own_grads, own_second, old_moment, stat_pieces, base_pieces, sent_bases, stat_piece,
     send, recv, local,
 ):
     place = Place()
-    half = ROWS // 2
-    mine = pl.ds(pl.multiple_of(place.core * half, half), half)
-    theirs = pl.ds(pl.multiple_of((1 - place.core) * half, half), half)
+    height = ROWS // SIDE // 2
 
     def quarter(p):
         return pl.ds(pl.multiple_of(p * (ROWS // SIDE), ROWS // SIDE), ROWS // SIDE)
@@ -313,7 +323,7 @@
                 (r.piece(base_right), base_pieces.at[1]),
                 (stat_left.at[stat_spot], stat_pieces.at[0]),
                 (stat_right.at[stat_spot], stat_pieces.at[1]),
-                (grads.at[mine, :], own_grads),
+                (grads.at[g.rows(place.p), :], own_grads),
                 (g.piece(moment), old_moment),
                 (second, own_second),
             )
@@ -331,6 +341,8 @@
     partners = [place.sibling(), place.far()]
     partners += [place.along_p(step) for step in (1, 2, 3)]
     partners += [place.along_q(step) for step in (1, 2, 3)]
+    partners += [place.across_p(step) for step in (1, 2, 3)]
+    partners += [place.across_q(step) for step in (1, 2, 3)]
     partners += [place.along_z(step) for step in range(1, SHARDS)]
     for partner in partners:
         pl.semaphore_signal(
@@ -347,7 +359,26 @@
     s_in = Ring(copies, stat_p_spot, place.along_p)
     s_out = Ring(copies, stat_q_spot, place.along_q)
 
-    core_copy = copies.start(grads.at[theirs, :], recv0, place.sibling())
+    def other_rows(p):
+        start = (1 - place.core) * (ROWS // 2) + p * height
+        return pl.ds(pl.multiple_of(start, height), height)
+
+    sum_copies = [
+        copies.start(
+            grads.at[g.rows(lax.rem(place.p + step, SIDE)), :],
+            recv1.at[step - 1],
+            place.along_p(step),
+        )
+        for step in (1, 3, 2)
+    ]
+    sum_copies += [
+        copies.start(
+            grads.at[other_rows(lax.rem(place.q + step, SIDE)), :],
+            recv1.at[3 + step],
+            place.across_q(step),
+        )
+        for step in (0, 1, 3, 2)
+    ]
     l.z_stage(sent_bases.at[0])
     r.z_stage(sent_bases.at[1])
     s_spread = Spread(
@@ -359,19 +390,12 @@
     )
 
     loads[4].wait()
-    core_copy.wait_recv()
-    acc0[...] = (
-        own_grads[...].astype(jnp.float32) + recv0[...].astype(jnp.float32)
-    ).reshape(acc0.shape)
-    p_copies = [
-        copies.start(
-            acc0.at[lax.rem(place.p + step, SIDE)], recv1.at[step - 1], place.along_p(step)
-        )
-        for step in (1, 3, 2)
-    ]
-    for copy in p_copies:
+    for copy in sum_copies:
         copy.wait_recv()
-    acc1[...] = (acc0[place.p] + recv1[0]) + (recv1[1] + recv1[2])
+    total = own_grads[...].astype(jnp.float32)
+    for index in range(7):
+        total = total + recv1[index].astype(jnp.float32)
+    acc1[...] = total
     q_copies = [
         copies.start(
             acc1.at[:, cols(lax.rem(place.q + step, SIDE))],
@@ -419,7 +443,6 @@
     m.q_third()
     r.finish()
     own = g.rows(place.p)
-    height = ROWS // SIDE // 2
     pair = jnp.concatenate(
         [all_grad[:, own, :].reshape(ROWS, ORDER), all_moment[:, own, :].reshape(ROWS, ORDER)]
     )
@@ -437,11 +460,13 @@
     g.finish()
     renew_stat(place, all_grad, all_stat, new_stat)
     s_out.first()
+    l.finish()
+    left_rot, right_rot, rot = bases.at[0], bases.at[1], bases.at[place.core]
+    for index in range(SIDE):
+        product[:, cols(index)] = quarter_product(place, new_stat, rot, (0,), index)
     t.p_third()
-    l.finish()
     t.finish()
     loads[6].wait()
-    left_rot, right_rot = bases.at[0], bases.at[1]
     rotate(left_rot, all_turned, own_second, out_second, scaled)
     s_out.second()
     turn_back(left_rot, scaled, back)
@@ -455,17 +480,18 @@
         for step in (7, 1, 6, 2, 5, 3, 4)
     ]
     back_rows[:, here] = back[place.z]
+    for index in range(SIDE):
+        product[:, cols(index)] += quarter_product(place, new_stat, rot, (1, 3), index)
     s_out.arrived()
-
-    rot = bases.at[place.core]
-    power_step(new_stat, rot, current)
+    for index in range(SIDE):
+        whole = product[:, cols(index)] + quarter_product(place, new_stat, rot, (2,), index)
+        current[:, :, cols(index)] = normalize(whole)
     for _ in range(NS_ITERS - 1):
         newton_schulz(current, gram, later)
         current, later = later, current
     rows = current[place.z]
 
-    @pl.loop(0, SIDE)
-    def _(index):
+    for index in range(SIDE):
         block = contract_cols(rows, rows_of(current, index)) / ORDER
         gram_rows[:, cols(index)] = block.astype(jnp.bfloat16)
 
@@ -481,8 +507,7 @@
     for copy in back_copies:
         copy.wait_recv()
 
-    @pl.loop(0, SIDE)
-    def _(index):
+    for index in range(SIDE):
         block = contract_cols(back_rows[...], rows_of(right_rot, index)) / ORDER
         out_update[:, cols(index)] = block.astype(jnp.bfloat16)
 
@@ -519,16 +544,15 @@
             pltpu.VMEM((ORDER, ROWS), bf16),
             pltpu.VMEM((SHARDS, ROWS, ROWS), bf16),
             pltpu.VMEM((ROWS, ORDER), bf16),
-            pltpu.VMEM((ROWS // 2, ORDER), bf16),
-            pltpu.VMEM((SIDE, height, ORDER), f32),
-            pltpu.VMEM((SIDE - 1, height, ORDER), f32),
+            pltpu.VMEM((ORDER, ORDER), f32),
+            pltpu.VMEM((7, height, ORDER), bf16),
             pltpu.VMEM((height, ORDER), f32),
             pltpu.VMEM((SIDE - 1, height, COLS), f32),
             pltpu.VMEM((height, COLS), f32),
             pltpu.VMEM((height, COLS), f32),
             pltpu.VMEM((height, COLS), bf16),
             pltpu.VMEM((height, COLS), bf16),
-            pltpu.VMEM((ROWS // 2, ORDER), bf16),
+            pltpu.VMEM((height, ORDER), bf16),
             pltpu.VMEM((ORDER, ROWS), f32),
             pltpu.VMEM((height, COLS), f32),
             pltpu.VMEM((2, 2 * height, COLS), f32),
@@ -544,11 +568,57 @@
     )(*operands)
 
 
+def deliver_kernel(
+    update, second, bases, out_update, out_second, out_left, out_right,
+    held_update, held_second, held_bases, sems_in, sems_out,
+):
+    routes = (
+        (bases.at[0], held_bases.at[0], out_left),
+        (bases.at[1], held_bases.at[1], out_right),
+        (second, held_second, out_second),
+        (update, held_update, out_update),
+    )
+    loads = [
+        pltpu.make_async_copy(src, held, sems_in.at[index])
+        for index, (src, held, _) in enumerate(routes)
+    ]
+    stores = [
+        pltpu.make_async_copy(held, dst, sems_out.at[index])
+        for index, (_, held, dst) in enumerate(routes)
+    ]
+    for load in loads:
+        load.start()
+    for load, store in zip(loads, stores):
+        load.wait()
+        store.start()
+    for store in stores:
+        store.wait()
+
+
+def deliver(update, second, bases):
+    one = jax.ShapeDtypeStruct(bases.shape[1:], bases.dtype)
+    outs = [jax.ShapeDtypeStruct(array.shape, array.dtype) for array in (update, second)]
+    return pl.pallas_call(
+        deliver_kernel,
+        out_shape=[*outs, one, one],
+        in_specs=[pl.BlockSpec(memory_space=pl.ANY)] * 3,
+        out_specs=[pl.BlockSpec(memory_space=pl.ANY)] * 4,
+        scratch_shapes=[
+            pltpu.VMEM(update.shape, update.dtype),
+            pltpu.VMEM(second.shape, second.dtype),
+            pltpu.VMEM(bases.shape, bases.dtype),
+            pltpu.SemaphoreType.DMA((4,)),
+            pltpu.SemaphoreType.DMA((4,)),
+        ],
+        name="deliver",
+    )(update, second, bases)
+
+
 def body(group_grads, moment, second, stat_left, stat_right, basis_left, basis_right):
     update, second_new, bases = step(
         group_grads[0], moment, second, stat_left, stat_right, basis_left, basis_right
     )
-    return (update, second_new, bases[0], bases[1])
+    return tuple(deliver(update, second_new, bases))
 
 
 def solution(mesh):

time: 106 us -> 102 us (0.962)
  local copies, waits for them, and re-layouts: 4.25 us -> 0 us
    pallas_call x0 -> x1, Pallas kernels: none -> 2.33 us  [deliver(): pl.pallas_call(deliver_kernel, out_shape=[*outs, one, one], in_specs=[pl....]
    squeeze x1 -> x0, local copies, waits for them, and re-layouts: 2.32 us -> none  [body(): return (update, second_new, bases[0], bases[1])]
    pallas_call x1, Pallas kernels: 99.8 us -> 97.6 us  [step(): pl.pallas_call(step_kernel, out_shape=[jax.ShapeDtypeStruct((ROWS, ORDER)...]
    unnamed x6 -> x0, local copies, waits for them, and re-layouts: 1.93 us -> none
where the time goes in v4:
time: 102 us; the launch traced here: 101 us
  Pallas kernels  99.9 us (98%)
    pallas_call x1, Pallas kernels, step(): pl.pallas_call(step_kernel, out_shape=[jax.ShapeDtypeStruct((ROWS, ORDER)...  97.6 us
    pallas_call x1, Pallas kernels, deliver(): pl.pallas_call(deliver_kernel, out_shape=[*outs, one, one], in_specs=[pl....  2.33 us

profile of v4, /device:TPU:1, one launch (start us, length us, event | category | flops | bytes accessed | tf_op | source)
XLA Modules:
  0.0 100.5 jit_solution(2418267418065187580)
XLA Ops:
  0.6 97.6 %step.1 = (bf16[128,1024]{1,0:T(8,128)(2,1)}, f32[1024,128]{1,0:T(8,128)}, f32[2,128,1024]{2,1,0:T(8,128)}) custom-call(bf16[128,1024]{1,0:T(8,128)(2,1)} %bitcast.1, f32[128,1024]{1,0:T(8,128)} %moment.1, f32[1024,128]{1,0:T(8,128)} %second.1, f32[128,1024]{1,0:T(8,128)} %stat_left.1, f32[128,1024]{1,0:T(8,128)} %stat_right.1, f32[128,1024]{1,0:T(8,128)} %base_left.1, ...), custom_call_target="tpu_custom_call" | custom-call | tf_op jit(solution)/shard_map/step/pallas_call | solution.py:524
  98.2 2.3 %deliver.1 = (bf16[128,1024]{1,0:T(8,128)(2,1)}, f32[1024,128]{1,0:T(8,128)}, f32[128,1024]{1,0:T(8,128)}, f32[128,1024]{1,0:T(8,128)}) custom-call(bf16[128,1024]{1,0:T(8,128)(2,1)} %get-tuple-element.7.update, f32[1024,128]{1,0:T(8,128)} %get-tuple-element.8.second, f32[2,128,1024]{2,1,0:T(8,128)} %get-tuple-element.9.bases), custom_call_target="tpu_custom_call" | custom-call | tf_op jit(solution)/shard_map/deliver/pallas_call | solution.py:601

commit v5 on v4

--- a/solution.py
+++ b/solution.py
@@ -229,15 +229,6 @@
         new = BETA_TWO * second[cols(index), :] + (1.0 - BETA_TWO) * grad_rot * grad_rot
         out_second[cols(index), :] = new
         scaled[cols(index), :] = (moment_rot / (jnp.sqrt(new) + EPSILON)).astype(jnp.bfloat16)
-
-
-def turn_back(left_rot, scaled, back):
-    for index in range(SIDE):
-        back[pl.ds(2 * index, 2)] = (
-            multiply(rows_of(left_rot, index), scaled[...])
-            .astype(jnp.bfloat16)
-            .reshape(2, ROWS, ROWS)
-        )
 
 
 def quarter_product(place, stat, rot, steps, index):
@@ -381,14 +372,6 @@
     ]
     l.z_stage(sent_bases.at[0])
     r.z_stage(sent_bases.at[1])
-    s_spread = Spread(
-        place,
-        copies,
-        stat_piece,
-        all_stat.at[place.z, quarter(place.p), :],
-        local.at[5],
-    )
-
     loads[4].wait()
     for copy in sum_copies:
         copy.wait_recv()
@@ -410,6 +393,8 @@
     far_copy = copies.start(acc2, recv3, place.far())
     l.q_first()
     r.q_first()
+    l.q_second()
+    r.q_second()
     far_copy.wait_recv()
     piece = (acc2[...] + recv3[...]).astype(jnp.bfloat16)
     grad_piece[...] = piece
@@ -419,27 +404,38 @@
         BETA_ONE * old + (1.0 - BETA_ONE) * piece.astype(jnp.float32)
     ).astype(jnp.bfloat16)
     g.z_stage(grad_piece)
+    s_spread = Spread(
+        place,
+        copies,
+        stat_piece,
+        all_stat.at[place.z, quarter(place.p), :],
+        local.at[5],
+    )
     m.z_stage(moment_piece)
 
-    l.q_second()
-    r.q_second()
     l.q_third()
     l.p_first()
     r.q_third()
     r.p_first()
+    l.p_second()
+    r.p_second()
+    g.q_first()
+    l.p_third()
+    r.p_third()
+    g.q_second()
+    g.q_third()
+    g.p_first()
+    g.p_second()
     s_spread.arrived()
     s_in.first()
-    g.q_first()
+    g.p_third()
     m.q_first()
-    r.p_second()
-    l.p_second()
     s_in.second()
-    g.q_second()
     m.q_second()
-    r.p_third()
-    l.p_third()
-    g.q_third()
-    g.p_first()
+    g.finish()
+    s_in.arrived()
+    renew_stat(place, all_grad, all_stat, new_stat)
+    s_out.first()
     m.q_third()
     r.finish()
     own = g.rows(place.p)
@@ -452,36 +448,35 @@
     ).astype(jnp.bfloat16)
     all_turned[:, own, :ROWS] = turned[:ROWS].reshape(SHARDS, height, ROWS)
     all_turned[:, own, ROWS:] = turned[ROWS:].reshape(SHARDS, height, ROWS)
-    g.p_second()
     t.p_first()
-    g.p_third()
-    t.p_second()
-    s_in.arrived()
-    g.finish()
-    renew_stat(place, all_grad, all_stat, new_stat)
-    s_out.first()
     l.finish()
     left_rot, right_rot, rot = bases.at[0], bases.at[1], bases.at[place.core]
     for index in range(SIDE):
         product[:, cols(index)] = quarter_product(place, new_stat, rot, (0,), index)
+    t.p_second()
+    s_out.second()
     t.p_third()
+    for index in range(SIDE):
+        product[:, cols(index)] += quarter_product(place, new_stat, rot, (1, 3), index)
     t.finish()
     loads[6].wait()
     rotate(left_rot, all_turned, own_second, out_second, scaled)
-    s_out.second()
-    turn_back(left_rot, scaled, back)
+    half_rows = pl.ds(pl.multiple_of(place.core * (ROWS // 2), ROWS // 2), ROWS // 2)
+    back[...] = (
+        multiply(left_rot[:, half_rows, :].reshape(ORDER // 2, ORDER), scaled[...])
+        .astype(jnp.bfloat16)
+        .reshape(SHARDS, ROWS // 2, ROWS)
+    )
     here = pl.ds(pl.multiple_of(place.z * ROWS, ROWS), ROWS)
     back_copies = [
         copies.start(
             back.at[lax.rem(place.z + step, SHARDS)],
-            back_rows.at[:, here],
+            back_rows.at[half_rows, here],
             place.along_z(step),
         )
         for step in (7, 1, 6, 2, 5, 3, 4)
     ]
-    back_rows[:, here] = back[place.z]
-    for index in range(SIDE):
-        product[:, cols(index)] += quarter_product(place, new_stat, rot, (1, 3), index)
+    back_rows[half_rows, here] = back[place.z]
     s_out.arrived()
     for index in range(SIDE):
         whole = product[:, cols(index)] + quarter_product(place, new_stat, rot, (2,), index)
@@ -489,6 +484,10 @@
     for _ in range(NS_ITERS - 1):
         newton_schulz(current, gram, later)
         current, later = later, current
+    for copy in back_copies:
+        copy.wait_recv()
+    share = back_rows.at[half_rows, :]
+    share_copy = copies.start(share, share, place.sibling())
     rows = current[place.z]
 
     for index in range(SIDE):
@@ -504,8 +503,7 @@
         block = out_bases.at[place.core, :, span]
         result_copies.append(copies.start(block, block, place.sibling()))
 
-    for copy in back_copies:
-        copy.wait_recv()
+    share_copy.wait_recv()
 
     for index in range(SIDE):
         block = contract_cols(back_rows[...], rows_of(right_rot, index)) / ORDER
@@ -542,7 +540,7 @@
             pltpu.VMEM(whole, bf16),
             pltpu.VMEM((ROWS, ORDER), bf16),
             pltpu.VMEM((ORDER, ROWS), bf16),
-            pltpu.VMEM((SHARDS, ROWS, ROWS), bf16),
+            pltpu.VMEM((SHARDS, ROWS // 2, ROWS), bf16),
             pltpu.VMEM((ROWS, ORDER), bf16),
             pltpu.VMEM((ORDER, ORDER), f32),
             pltpu.VMEM((7, height, ORDER), bf16),

time: 102 us -> 103 us (level); the launches traced: 101 us -> 103 us
  Pallas kernels: 99.9 us -> 102 us
    pallas_call x1, Pallas kernels: 97.6 us -> 99.6 us  [step(): pl.pallas_call(step_kernel, out_shape=[jax.ShapeDtypeStruct((ROWS, ORDER)...]
where the time goes in v5:
time: 103 us
  Pallas kernels  102 us (99%)
    pallas_call x1, Pallas kernels, step(): pl.pallas_call(step_kernel, out_shape=[jax.ShapeDtypeStruct((ROWS, ORDER)...  99.6 us
    pallas_call x1, Pallas kernels, deliver(): pl.pallas_call(deliver_kernel, out_shape=[*outs, one, one], in_specs=[pl....  2.33 us

profile of v5, /device:TPU:1, one launch (start us, length us, event | category | flops | bytes accessed | tf_op | source)
XLA Modules:
  0.0 102.6 jit_solution(7483344166591944364)
XLA Ops:
  0.6 99.6 %step.1 = (bf16[128,1024]{1,0:T(8,128)(2,1)}, f32[1024,128]{1,0:T(8,128)}, f32[2,128,1024]{2,1,0:T(8,128)}) custom-call(bf16[128,1024]{1,0:T(8,128)(2,1)} %bitcast.1, f32[128,1024]{1,0:T(8,128)} %moment.1, f32[1024,128]{1,0:T(8,128)} %second.1, f32[128,1024]{1,0:T(8,128)} %stat_left.1, f32[128,1024]{1,0:T(8,128)} %stat_right.1, f32[128,1024]{1,0:T(8,128)} %base_left.1, ...), custom_call_target="tpu_custom_call" | custom-call | tf_op jit(solution)/shard_map/step/pallas_call | solution.py:522
  100.2 2.3 %deliver.1 = (bf16[128,1024]{1,0:T(8,128)(2,1)}, f32[1024,128]{1,0:T(8,128)}, f32[128,1024]{1,0:T(8,128)}, f32[128,1024]{1,0:T(8,128)}) custom-call(bf16[128,1024]{1,0:T(8,128)(2,1)} %get-tuple-element.7.update, f32[1024,128]{1,0:T(8,128)} %get-tuple-element.8.second, f32[2,128,1024]{2,1,0:T(8,128)} %get-tuple-element.9.bases), custom_call_target="tpu_custom_call" | custom-call | tf_op jit(solution)/shard_map/deliver/pallas_call | solution.py:599

commit v6 on v5

--- a/solution.py
+++ b/solution.py
@@ -404,6 +404,7 @@
         BETA_ONE * old + (1.0 - BETA_ONE) * piece.astype(jnp.float32)
     ).astype(jnp.bfloat16)
     g.z_stage(grad_piece)
+    m.z_stage(moment_piece)
     s_spread = Spread(
         place,
         copies,
@@ -411,7 +412,6 @@
         all_stat.at[place.z, quarter(place.p), :],
         local.at[5],
     )
-    m.z_stage(moment_piece)
 
     l.q_third()
     l.p_first()
@@ -420,22 +420,13 @@
     l.p_second()
     r.p_second()
     g.q_first()
+    m.q_first()
     l.p_third()
     r.p_third()
     g.q_second()
+    m.q_second()
     g.q_third()
     g.p_first()
-    g.p_second()
-    s_spread.arrived()
-    s_in.first()
-    g.p_third()
-    m.q_first()
-    s_in.second()
-    m.q_second()
-    g.finish()
-    s_in.arrived()
-    renew_stat(place, all_grad, all_stat, new_stat)
-    s_out.first()
     m.q_third()
     r.finish()
     own = g.rows(place.p)
@@ -449,17 +440,21 @@
     all_turned[:, own, :ROWS] = turned[:ROWS].reshape(SHARDS, height, ROWS)
     all_turned[:, own, ROWS:] = turned[ROWS:].reshape(SHARDS, height, ROWS)
     t.p_first()
+    g.p_second()
+    s_spread.arrived()
+    s_in.first()
+    t.p_second()
+    g.p_third()
+    s_in.second()
+    t.p_third()
+    g.finish()
+    s_in.arrived()
+    renew_stat(place, all_grad, all_stat, new_stat)
+    s_out.first()
     l.finish()
-    left_rot, right_rot, rot = bases.at[0], bases.at[1], bases.at[place.core]
-    for index in range(SIDE):
-        product[:, cols(index)] = quarter_product(place, new_stat, rot, (0,), index)
-    t.p_second()
-    s_out.second()
-    t.p_third()
-    for index in range(SIDE):
-        product[:, cols(index)] += quarter_product(place, new_stat, rot, (1, 3), index)
     t.finish()
     loads[6].wait()
+    left_rot, right_rot, rot = bases.at[0], bases.at[1], bases.at[place.core]
     rotate(left_rot, all_turned, own_second, out_second, scaled)
     half_rows = pl.ds(pl.multiple_of(place.core * (ROWS // 2), ROWS // 2), ROWS // 2)
     back[...] = (
@@ -477,6 +472,11 @@
         for step in (7, 1, 6, 2, 5, 3, 4)
     ]
     back_rows[half_rows, here] = back[place.z]
+    for index in range(SIDE):
+        product[:, cols(index)] = quarter_product(place, new_stat, rot, (0,), index)
+    s_out.second()
+    for index in range(SIDE):
+        product[:, cols(index)] += quarter_product(place, new_stat, rot, (1, 3), index)
     s_out.arrived()
     for index in range(SIDE):
         whole = product[:, cols(index)] + quarter_product(place, new_stat, rot, (2,), index)

time: 103 us -> 104 us (level)
  no operation moved by 1% of the time
where the time goes in v6:
time: 104 us; the launch traced here: 103 us
  Pallas kernels  103 us (99%)
    pallas_call x1, Pallas kernels, step(): pl.pallas_call(step_kernel, out_shape=[jax.ShapeDtypeStruct((ROWS, ORDER)...  100 us
    pallas_call x1, Pallas kernels, deliver(): pl.pallas_call(deliver_kernel, out_shape=[*outs, one, one], in_specs=[pl....  2.33 us

profile of v6, /device:TPU:1, one launch (start us, length us, event | category | flops | bytes accessed | tf_op | source)
XLA Modules:
  0.0 103.4 jit_solution(15911925832745812741)
XLA Ops:
  0.6 100.3 %step.1 = (bf16[128,1024]{1,0:T(8,128)(2,1)}, f32[1024,128]{1,0:T(8,128)}, f32[2,128,1024]{2,1,0:T(8,128)}) custom-call(bf16[128,1024]{1,0:T(8,128)(2,1)} %bitcast.1, f32[128,1024]{1,0:T(8,128)} %moment.1, f32[1024,128]{1,0:T(8,128)} %second.1, f32[128,1024]{1,0:T(8,128)} %stat_left.1, f32[128,1024]{1,0:T(8,128)} %stat_right.1, f32[128,1024]{1,0:T(8,128)} %base_left.1, ...), custom_call_target="tpu_custom_call" | custom-call | tf_op jit(solution)/shard_map/step/pallas_call | solution.py:522
  100.9 2.3 %deliver.1 = (bf16[128,1024]{1,0:T(8,128)(2,1)}, f32[1024,128]{1,0:T(8,128)}, f32[128,1024]{1,0:T(8,128)}, f32[128,1024]{1,0:T(8,128)}) custom-call(bf16[128,1024]{1,0:T(8,128)(2,1)} %get-tuple-element.7.update, f32[1024,128]{1,0:T(8,128)} %get-tuple-element.8.second, f32[2,128,1024]{2,1,0:T(8,128)} %get-tuple-element.9.bases), custom_call_target="tpu_custom_call" | custom-call | tf_op jit(solution)/shard_map/deliver/pallas_call | solution.py:599

commit v7 on v6

--- a/solution.py
+++ b/solution.py
@@ -19,7 +19,7 @@
 ROWS = ORDER // SHARDS
 SIDE = 4
 COLS = ORDER // SIDE
-COPIES = 120
+COPIES = 150
 LOCALS = 13
 
 
@@ -105,23 +105,29 @@
     def __init__(self, copies, spot, along):
         self.copies, self.spot, self.along = copies, spot, along
 
+    def send(self, step, zs, to):
+        part = self.spot(step, zs)
+        return self.copies.start(part, part, self.along(to))
+
     def first(self):
-        own = self.spot(0, pl.ds(0, SHARDS))
-        self.stage = [
-            self.copies.start(own, own, self.along(1)),
-            self.copies.start(own, own, self.along(3)),
-        ]
+        low, high = pl.ds(0, SHARDS // 2), pl.ds(SHARDS // 2, SHARDS // 2)
+        self.early = [self.send(0, low, 1), self.send(0, high, 3)]
+        self.late = [self.send(0, high, 1), self.send(0, low, 3)]
 
     def second(self):
-        self.arrived()
         low, high = pl.ds(0, SHARDS // 2), pl.ds(SHARDS // 2, SHARDS // 2)
-        self.stage = [
-            self.copies.start(self.spot(3, low), self.spot(3, low), self.along(1)),
-            self.copies.start(self.spot(1, high), self.spot(1, high), self.along(3)),
-        ]
+        for copy in self.early:
+            copy.wait_recv()
+        self.last = [self.send(3, low, 1), self.send(1, high, 3)]
+
+    def near(self):
+        for copy in self.late:
+            copy.wait_recv()
+        self.late = []
 
     def arrived(self):
-        for copy in self.stage:
+        self.near()
+        for copy in self.last:
             copy.wait_recv()
 
 
@@ -183,6 +189,7 @@
 
     def p_second(self):
         self.p_ring.second()
+        self.p_ring.near()
         self.share(1)
         self.share(3)
 
@@ -475,6 +482,7 @@
     for index in range(SIDE):
         product[:, cols(index)] = quarter_product(place, new_stat, rot, (0,), index)
     s_out.second()
+    s_out.near()
     for index in range(SIDE):
         product[:, cols(index)] += quarter_product(place, new_stat, rot, (1, 3), index)
     s_out.arrived()

time: 104 us -> 97.8 us (0.940)
  Pallas kernels: 103 us -> 96.8 us
    pallas_call x1, Pallas kernels: 100 us -> 94.5 us  [step(): pl.pallas_call(step_kernel, out_shape=[jax.ShapeDtypeStruct((ROWS, ORDER)...]
where the time goes in v7:
time: 97.8 us; the launch traced here: 97.6 us
  Pallas kernels  96.8 us (99%)
    pallas_call x1, Pallas kernels, step(): pl.pallas_call(step_kernel, out_shape=[jax.ShapeDtypeStruct((ROWS, ORDER)...  94.5 us
    pallas_call x1, Pallas kernels, deliver(): pl.pallas_call(deliver_kernel, out_shape=[*outs, one, one], in_specs=[pl....  2.33 us

profile of v7, /device:TPU:1, one launch (start us, length us, event | category | flops | bytes accessed | tf_op | source)
XLA Modules:
  0.0 97.6 jit_solution(3395941106926542595)
XLA Ops:
  0.6 94.5 %step.1 = (bf16[128,1024]{1,0:T(8,128)(2,1)}, f32[1024,128]{1,0:T(8,128)}, f32[2,128,1024]{2,1,0:T(8,128)}) custom-call(bf16[128,1024]{1,0:T(8,128)(2,1)} %bitcast.1, f32[128,1024]{1,0:T(8,128)} %moment.1, f32[1024,128]{1,0:T(8,128)} %second.1, f32[128,1024]{1,0:T(8,128)} %stat_left.1, f32[128,1024]{1,0:T(8,128)} %stat_right.1, f32[128,1024]{1,0:T(8,128)} %base_left.1, ...), custom_call_target="tpu_custom_call" | custom-call | tf_op jit(solution)/shard_map/step/pallas_call | solution.py:530
  95.1 2.3 %deliver.1 = (bf16[128,1024]{1,0:T(8,128)(2,1)}, f32[1024,128]{1,0:T(8,128)}, f32[128,1024]{1,0:T(8,128)}, f32[128,1024]{1,0:T(8,128)}) custom-call(bf16[128,1024]{1,0:T(8,128)(2,1)} %get-tuple-element.7.update, f32[1024,128]{1,0:T(8,128)} %get-tuple-element.8.second, f32[2,128,1024]{2,1,0:T(8,128)} %get-tuple-element.9.bases), custom_call_target="tpu_custom_call" | custom-call | tf_op jit(solution)/shard_map/deliver/pallas_call | solution.py:607
